TPU v7x, 256 devices: a whole 4x4x8 slice. The times are simulated.
256 devices in a mesh: shot: 16 (over y, x), rcv: 16 (over z, core).
Axes of the slice: x: 4, y: 4, z: 8, core: 2. Of those that a mesh axis runs over, the one named last changes fastest.
Arguments:
- estimate: bfloat16 [512, 256, 512], P('shot', 'rcv'), may hold values from -6 to 6
- record: float32 [256, 65536], P('rcv', 'shot'), may hold values from -9 to 9
- fire_times: int32 [512], P('shot'), may hold values from 0 to 65535, as said below
- rcv_delay: int32 [256], P('rcv'), may hold values from 0 to 63, as said below
- threshold: float32 [256], replicated, may hold values from 0.2 to 1.5
Outputs:
- deblended: bfloat16 [512, 256, 512], P('shot', 'rcv')
Inputs may be any that keep to these rules, and one draw needn't show every extreme that they name: `fire_times`: shot s fires at a sample from s * 128 to s * 128 + 127; the first shot fires at 0 and the last at the last sample of its range. `rcv_delay`: the first receiver has the largest delay.
All inputs are finite; a program needn't handle non-finite values.
Results may differ from a plain program's by a relative error of at most 0.0068.
Values may be sent and summed in bfloat16 or wider, within the bound.
No kernel may reach another device: no remote copies, remote signals or barrier semaphores. Data moves between devices by JAX's collectives and lax.ppermute only.
A program may use at most 64 MiB of HBM per device.

v0:
```python
import math

import jax
import jax.numpy as jnp
from jax import lax
from jax.sharding import PartitionSpec as P

SHOTS = 512
PERIOD = 128
DRIFT = 64


def passed_along(value, axis, by):
    length = lax.axis_size(axis)
    return lax.ppermute(value, axis, [(i, (i + by) % length) for i in range(length)])


def time_tables(sample_count):
    freq_count = sample_count // 2
    samples = jnp.arange(sample_count, dtype=jnp.int32)
    freq_ids = jnp.arange(freq_count, dtype=jnp.int32)
    phases = samples[:, None] * freq_ids[None, :] % sample_count
    angles = phases.astype(jnp.float32) * (2.0 * math.pi / sample_count)
    factor = 1.0 / math.sqrt(sample_count)
    cosines = jnp.cos(angles) * factor
    sines = jnp.sin(angles) * factor
    forward = jnp.stack([cosines, -sines], axis=1).astype(jnp.bfloat16)
    weights = jnp.where(freq_ids == 0, 1.0, 2.0).astype(jnp.float32)
    inverse = jnp.stack(
        [(cosines * weights[None, :]).T, (-sines * weights[None, :]).T], axis=0
    ).astype(jnp.bfloat16)
    return (forward, inverse)


def shot_tables(shot_count):
    shot_ids = jnp.arange(shot_count, dtype=jnp.int32)
    phases = shot_ids[:, None] * shot_ids[None, :] % shot_count
    angles = phases.astype(jnp.float32) * (2.0 * math.pi / shot_count)
    factor = 1.0 / math.sqrt(shot_count)
    return (
        (jnp.cos(angles) * factor).astype(jnp.bfloat16),
        (jnp.sin(angles) * factor).astype(jnp.bfloat16),
    )


def shards(estimate, record, fire_times, rcv_delay, threshold):
    shot_count, rcv_count, sample_count = estimate.shape
    forward, inverse = time_tables(sample_count)
    cos_table, sin_table = shot_tables(SHOTS)
    spectrum = jnp.einsum(
        "srt,tcf->csrf", estimate, forward, preferred_element_type=jnp.float32
    ).astype(jnp.bfloat16)
    gathered = lax.all_to_all(spectrum, "shot", split_axis=2, concat_axis=1, tiled=True)
    fk_real = jnp.einsum("ks,srf->krf", cos_table, gathered[0], preferred_element_type=jnp.float32)
    fk_real = fk_real + jnp.einsum(
        "ks,srf->krf", sin_table, gathered[1], preferred_element_type=jnp.float32
    )
    fk_imag = jnp.einsum("ks,srf->krf", cos_table, gathered[1], preferred_element_type=jnp.float32)
    fk_imag = fk_imag - jnp.einsum(
        "ks,srf->krf", sin_table, gathered[0], preferred_element_type=jnp.float32
    )
    wavenumber = jnp.stack([fk_real, fk_imag], axis=0)
    magnitude = jnp.sqrt(wavenumber[0] * wavenumber[0] + wavenumber[1] * wavenumber[1] + 1e-12)
    level = threshold[None, None, :]
    factor = jnp.maximum(magnitude - level, 0.0) / jnp.maximum(magnitude, level)
    shrunk = (wavenumber * factor[None]).astype(jnp.bfloat16)
    back_real = jnp.einsum("ks,krf->srf", cos_table, shrunk[0], preferred_element_type=jnp.float32)
    back_real = back_real - jnp.einsum(
        "ks,krf->srf", sin_table, shrunk[1], preferred_element_type=jnp.float32
    )
    back_imag = jnp.einsum("ks,krf->srf", sin_table, shrunk[0], preferred_element_type=jnp.float32)
    back_imag = back_imag + jnp.einsum(
        "ks,krf->srf", cos_table, shrunk[1], preferred_element_type=jnp.float32
    )
    back = jnp.stack([back_real, back_imag], axis=0).astype(jnp.bfloat16)
    far_traces = jnp.einsum("csrf,cft->srt", back, inverse, preferred_element_type=jnp.float32)
    denoised = lax.all_to_all(far_traces, "shot", split_axis=0, concat_axis=1, tiled=True)
    block_len = shot_count * PERIOD
    rim_len = sample_count + DRIFT
    starts = fire_times % block_len
    placed_len = block_len + sample_count + 2 * DRIFT

    def place_shot(index, buffer):
        piece = lax.dynamic_index_in_dim(denoised, index, 0, keepdims=False)
        where = starts[index] + DRIFT
        current = lax.dynamic_slice_in_dim(buffer, where, sample_count, 1)
        return lax.dynamic_update_slice_in_dim(buffer, current + piece, where, 1)

    placed = lax.fori_loop(
        0, shot_count, place_shot, jnp.zeros((rcv_count, placed_len), jnp.float32)
    )

    def delay_row(row, delay):
        return lax.dynamic_slice_in_dim(row, DRIFT - delay, block_len + rim_len, 0)

    own_terms = jax.vmap(delay_row)(placed, rcv_delay)
    spill_part = passed_along(own_terms[:, block_len:].astype(jnp.bfloat16), "shot", 1).astype(
        jnp.float32
    )
    summed = own_terms[:, :block_len].at[:, :rim_len].add(spill_part)
    next_record, next_summed = passed_along((record[:, :rim_len], summed[:, :rim_len]), "shot", -1)
    record_ext = jnp.concatenate([record, next_record], axis=1)
    summed_ext = jnp.concatenate([summed, next_summed], axis=1)
    difference = record_ext - summed_ext

    def advance_row(row, delay):
        return lax.dynamic_slice_in_dim(row, delay, block_len + sample_count, 0)

    aligned = jax.vmap(advance_row)(difference, rcv_delay)

    def shot_window(start):
        return lax.dynamic_slice_in_dim(aligned, start, sample_count, 1)

    residual = jax.vmap(shot_window)(starts)
    return (denoised + 0.5 * residual).astype(jnp.bfloat16)


def solution(mesh):
    in_specs = (P("shot", "rcv", None), P("rcv", "shot"), P("shot"), P("rcv"), P())
    out_specs = P("shot", "rcv", None)
    return jax.shard_map(shards, mesh=mesh, in_specs=in_specs, out_specs=out_specs, check_vma=False)
```

profile of v0, /device:TPU:160, one launch (start us, length us, event | category | flops | bytes accessed | tf_op | source)
XLA Modules:
  0.0 300.2 jit_solution(13524281744578120527)
XLA Ops:
  0.0 2.2 negate_convert_fusion
  3.5 7.0 %all-to-all-start = ((bf16[2,32,16,256]{3,1,0,2:T(8,128)(2,1)}), bf16[2,32,16,256]{3,1,0,2:T(8,128)(2,1)S(1)}, u32[]{:S(2)}, u32[]{:S(2)}) async-start(bf16[2,32,16,256]{3,1,0,2:T(8,128)(2,1)} %copy.9), calls=%async_computation | async-start | bytes 1048576 | tf_op jit(solution)/shard_map/all_to_all | solution.py:53
  10.6 2.3 multiply_convert_fusion.2
  12.8 9.3 %all-to-all-done = bf16[2,32,16,256]{3,1,0,2:T(8,128)(2,1)S(1)} async-done(((bf16[2,32,16,256]{3,1,0,2:T(8,128)(2,1)}), bf16[2,32,16,256]{3,1,0,2:T(8,128)(2,1)S(1)}, u32[]{:S(2)}, u32[]{:S(2)}) %all-to-all-start) | async-done | bytes 524320 | tf_op jit(solution)/shard_map/all_to_all | solution.py:53
  22.1 5.1 %fusion.34 = f32[512,256]{1,0:T(8,128)S(1)} fusion(bf16[512,256]{1,0:T(8,128)(2,1)S(1)} %bitcast.85), kind=kOutput, calls=%fused_computation.65 | convolution fusion | flops 138412032 | bytes 786432 | tf_op jit(solution)/shard_map/ks,srf->krf/dot_general | solution.py:54
  27.2 5.1 %fusion.33 = f32[512,256]{1,0:T(8,128)S(1)} fusion(bf16[512,256]{1,0:T(8,128)(2,1)S(1)} %bitcast.87), kind=kOutput, calls=%fused_computation.64 | convolution fusion | flops 138412032 | bytes 786432 | tf_op jit(solution)/shard_map/ks,srf->krf/dot_general | solution.py:58
  32.3 5.3 %convolution_add_fusion.1 = f32[512,256]{1,0:T(8,128)S(1)} fusion(f32[512,256]{1,0:T(8,128)S(1)} %fusion.34, bf16[512,256]{1,0:T(8,128)(2,1)S(1)} %bitcast.88), kind=kOutput, calls=%fused_computation.14 | convolution fusion | flops 138543104 | bytes 1310720 | tf_op jit(solution)/shard_map/ks,srf->krf/dot_general | solution.py:55
  37.6 4.3 %maximum_divide_fusion = (f32[512,256]{1,0:T(8,128)S(1)}, f32[512,256]{1,0:T(8,128)S(1)}) fusion(f32[512,256]{1,0:T(8,128)S(1)} %convolution_add_fusion.1, f32[256]{0:T(256)S(1)} %copy-done.2, f32[512,256]{1,0:T(8,128)S(1)} %fusion.33, bf16[512,256]{1,0:T(8,128)(2,1)S(1)} %bitcast.86), kind=kOutput, calls=%fused_computation.58 | convolution fusion | flops 139591680 | bytes 2360320 | tf_op jit(solution)/shard_map/ks,srf->krf/dot_general | solution.py:59
  42.1 4.0 %fusion.32 = f32[512,256]{1,0:T(8,128)S(1)} fusion(bf16[2,512,1,256]{3,1,2,0:T(8,128)(2,1)S(1)} %fusion.8), kind=kOutput, calls=%fused_computation.63 | convolution fusion | flops 138412032 | bytes 786432 | tf_op jit(solution)/shard_map/ks,krf->srf/dot_general | solution.py:67
  46.1 4.3 %fusion.35 = f32[512,256]{1,0:T(8,128)S(1)} fusion(bf16[2,512,1,256]{3,1,2,0:T(8,128)(2,1)S(1)} %fusion.8), kind=kOutput, calls=%fused_computation.66 | convolution fusion | flops 138412032 | bytes 786432 | tf_op jit(solution)/shard_map/ks,krf->srf/dot_general | solution.py:71
  50.4 4.4 %fusion.4 = bf16[1,512,256]{2,1,0:T(8,128)(2,1)S(1)} fusion(f32[512,256]{1,0:T(8,128)S(1)} %fusion.32, bf16[2,512,1,256]{3,1,2,0:T(8,128)(2,1)S(1)} %fusion.8), kind=kOutput, calls=%fused_computation.18 | convolution fusion | flops 138674176 | bytes 1048576 | tf_op jit(solution)/shard_map/ks,krf->srf/dot_general | solution.py:68
  54.8 4.3 %fusion.3 = bf16[1,512,256]{2,1,0:T(8,128)(2,1)S(1)} fusion(f32[512,256]{1,0:T(8,128)S(1)} %fusion.35, bf16[2,512,1,256]{3,1,2,0:T(8,128)(2,1)S(1)} %fusion.8), kind=kOutput, calls=%fused_computation.17 | convolution fusion | flops 138674176 | bytes 1048576 | tf_op jit(solution)/shard_map/ks,krf->srf/dot_general | solution.py:72
  59.6 2.1 copy.10
  61.6 3.7 %all-to-all-start.1 = ((f32[512,1,512]{2,1,0:T(1,128)}), f32[512,1,512]{2,1,0:T(1,128)S(1)}, u32[]{:S(2)}, u32[]{:S(2)}) async-start(f32[512,1,512]{2,1,0:T(1,128)} %copy.10), calls=%async_computation.1 | async-start | bytes 2097152 | tf_op jit(solution)/shard_map/all_to_all | solution.py:77
  66.6 15.0 %all-to-all-done.1 = f32[512,1,512]{2,1,0:T(1,128)S(1)} async-done(((f32[512,1,512]{2,1,0:T(1,128)}), f32[512,1,512]{2,1,0:T(1,128)S(1)}, u32[]{:S(2)}, u32[]{:S(2)}) %all-to-all-start.1) | async-done | bytes 1048608 | tf_op jit(solution)/shard_map/all_to_all | solution.py:77
  82.3 82.2 %while.19 = (s32[]{:T(128)}, f32[16,4736]{1,0:T(8,128)S(1)}, s32[32]{0:T(128)S(1)}, f32[32,16,512]{2,1,0:T(8,128)S(1)}, s32[]{:T(128)}, /*index=5*/s32[1]{0:T(128)}, s32[]{:T(128)}, s32[1]{0:T(128)}) while((s32[]{:T(128)}, f32[16,4736]{1,0:T(8,128)S(1)}, s32[32]{0:T(128)S(1)}, f32[32,16,512]{2,1,0:T(8,128)S(1)}, s32[]{:T(128)}, ...), condition=%wide.region_1.2_spmd, body=%wide.region_0.1_spmd.sunk | while | flops 8198 | bytes 163995 | solution.py:89
  164.5 39.9 %while.20 = (s32[]{:T(128)}, f32[16,4736]{1,0:T(8,128)S(1)}, s32[16,2]{0,1:T(2,128)S(1)}, f32[16,4672]{1,0:T(8,128)S(1)}, s32[]{:T(128)}, /*index=5*/s32[]{:T(128)}) while((s32[]{:T(128)}, f32[16,4736]{1,0:T(8,128)S(1)}, s32[16,2]{0,1:T(2,128)S(1)}, f32[16,4672]{1,0:T(8,128)S(1)}, s32[]{:T(128)}, /*index=5*/s32[]{:T(128)}) %tuple.89), condition=%wide.while_cond.1, body=%wide.while_body.1.sunk | while | flops 2 | bytes 74865 | solution.py:94
  165.2 1.4 dynamic-slice.29
  167.7 1.4 dynamic-slice.29
  170.2 1.4 dynamic-slice.29
  172.7 1.4 dynamic-slice.29
  175.2 1.4 dynamic-slice.29
  177.7 1.4 dynamic-slice.29
  180.2 1.4 dynamic-slice.29
  182.7 1.4 dynamic-slice.29
  185.2 1.4 dynamic-slice.29
  187.7 1.4 dynamic-slice.29
  190.2 1.4 dynamic-slice.29
  192.7 1.4 dynamic-slice.29
  195.1 1.4 dynamic-slice.29
  197.6 1.4 dynamic-slice.29
  200.1 1.4 dynamic-slice.29
  202.6 1.4 dynamic-slice.29
  205.2 4.7 %collective-permute-start = (f32[16,576]{1,0:T(8,128)S(1)}, f32[16,576]{1,0:T(8,128)S(1)}, u32[]{:S(2)}, u32[]{:S(2)}) collective-permute-start(f32[16,576]{1,0:T(8,128)S(1)} %slice.55), channel_id=1, source_target_pairs={{0,240},{16,0},{32,16},{48,32},{64,48},{80,64},{96,80},{112,96},{1... | collective-permute-start | bytes 110600 | tf_op jit(solution)/shard_map/ppermute | solution.py:15
  213.0 3.4 %collective-permute-done.2 = f32[16,576]{1,0:T(8,128)S(1)} collective-permute-done((f32[16,576]{1,0:T(8,128)S(1)}, f32[16,576]{1,0:T(8,128)S(1)}, u32[]{:S(2)}, u32[]{:S(2)}) %collective-permute-start.2) | collective-permute-done | bytes 36896 | tf_op jit(solution)/shard_map/ppermute | solution.py:15
  216.4 39.7 %while.21 = (s32[]{:T(128)}, f32[16,4672]{1,0:T(8,128)S(1)}, s32[16,2]{0,1:T(2,128)S(1)}, f32[16,4608]{1,0:T(8,128)S(1)}, s32[]{:T(128)}, /*index=5*/s32[]{:T(128)}) while((s32[]{:T(128)}, f32[16,4672]{1,0:T(8,128)S(1)}, s32[16,2]{0,1:T(2,128)S(1)}, f32[16,4608]{1,0:T(8,128)S(1)}, s32[]{:T(128)}, /*index=5*/s32[]{:T(128)}) %tuple.92), condition=%wide.while_cond.2, body=%wide.while_body.2.sunk | while | flops 2 | bytes 73841 | solution.py:107
  217.1 1.4 dynamic-slice.31
  219.6 1.4 dynamic-slice.31
  222.0 1.4 dynamic-slice.31
  224.5 1.4 dynamic-slice.31
  227.0 1.4 dynamic-slice.31
  229.5 1.4 dynamic-slice.31
  232.0 1.4 dynamic-slice.31
  234.5 1.4 dynamic-slice.31
  236.9 1.4 dynamic-slice.31
  241.9 1.4 dynamic-slice.31
  256.1 42.6 %while.22 = (s32[]{:T(128)}, f32[16,4608]{1,0:T(8,128)S(1)}, s32[32,2]{0,1:T(2,128)S(1)}, f32[32,16,512]{2,1,0:T(8,128)S(1)}, s32[]{:T(128)}) while((s32[]{:T(128)}, f32[16,4608]{1,0:T(8,128)S(1)}, s32[32,2]{0,1:T(2,128)S(1)}, f32[32,16,512]{2,1,0:T(8,128)S(1)}, s32[]{:T(128)}) %tuple.95), condition=%wide.while_cond.3, body=%wide.while_body.3.sunk | while | flops 2 | bytes 65633 | solution.py:112
  298.7 1.5 add_convert_fusion
  (332 shorter events, 134.9 us)
Async XLA Ops:
  0.0 2.2 copy-start.1
  3.5 18.6 %all-to-all-start = ((bf16[2,32,16,256]{3,1,0,2:T(8,128)(2,1)}), bf16[2,32,16,256]{3,1,0,2:T(8,128)(2,1)S(1)}, u32[]{:S(2)}, u32[]{:S(2)}) async-start(bf16[2,32,16,256]{3,1,0,2:T(8,128)(2,1)} %copy.9), calls=%async_computation | async-start | bytes 1048576 | tf_op jit(solution)/shard_map/all_to_all | solution.py:53
  32.3 5.3 %copy-start.2 = (f32[256]{0:T(256)S(1)}, f32[256]{0:T(256)}, u32[]{:S(2)}) copy-start(f32[256]{0:T(256)} %param.13) | copy-start | bytes 3076
  61.6 20.0 %all-to-all-start.1 = ((f32[512,1,512]{2,1,0:T(1,128)}), f32[512,1,512]{2,1,0:T(1,128)S(1)}, u32[]{:S(2)}, u32[]{:S(2)}) async-start(f32[512,1,512]{2,1,0:T(1,128)} %copy.10), calls=%async_computation.1 | async-start | bytes 2097152 | tf_op jit(solution)/shard_map/all_to_all | solution.py:77
  65.3 0.7 copy-start.3
  66.0 0.7 copy-start.4
  82.3 122.9 %copy-start = (f32[16,4096]{1,0:T(8,128)S(1)}, f32[16,4096]{1,0:T(8,128)}, u32[]{:S(2)}) copy-start(f32[16,4096]{1,0:T(8,128)} %param.10) | copy-start | bytes 786436
  204.5 7.2 %collective-permute-start.1 = (bf16[16,576]{1,0:T(8,128)(2,1)S(1)}, bf16[16,576]{1,0:T(8,128)(2,1)S(1)}, u32[]{:S(2)}, u32[]{:S(2)}) collective-permute-start(bf16[16,576]{1,0:T(8,128)(2,1)S(1)} %slice.105), channel_id=1, source_target_pairs={{0,16},{16,32},{32,48},{48,64},{64,80},{80,96},{96,112},{112,128},... | collective-permute-start | bytes 55304 | tf_op jit(solution)/shard_map/ppermute | solution.py:15
  205.2 7.8 %collective-permute-start = (f32[16,576]{1,0:T(8,128)S(1)}, f32[16,576]{1,0:T(8,128)S(1)}, u32[]{:S(2)}, u32[]{:S(2)}) collective-permute-start(f32[16,576]{1,0:T(8,128)S(1)} %slice.55), channel_id=1, source_target_pairs={{0,240},{16,0},{32,16},{48,32},{64,48},{80,64},{96,80},{112,96},{1... | collective-permute-start | bytes 110600 | tf_op jit(solution)/shard_map/ppermute | solution.py:15
  212.3 4.1 %collective-permute-start.2 = (f32[16,576]{1,0:T(8,128)S(1)}, f32[16,576]{1,0:T(8,128)S(1)}, u32[]{:S(2)}, u32[]{:S(2)}) collective-permute-start(f32[16,576]{1,0:T(8,128)S(1)} %add_select_fusion.3), channel_id=1, source_target_pairs={{0,240},{16,0},{32,16},{48,32},{64,48},{80,64},{96,80},{112,96},{1... | collective-permute-start | bytes 110600 | tf_op jit(solution)/shard_map/ppermute | solution.py:15
where the time goes:
time: 302 us; the launch traced here: 300 us
  local copies, waits for them, and re-layouts  165 us (55%)
  loops' own time  41.9 us (14%)
  matrix products  37.7 us (12%)
  waiting for transfers between devices  28.7 us (10%)
  starting transfers between devices  16.2 us (5%)
  other arithmetic  10.1 us (3%)
    gather x224, local copies, waits for them, and re-layouts  121 us
    another operation x1, loops' own time, shards(): lax.fori_loop(0, shot_count, place_shot, jnp.zeros((rcv_count, placed_len...  40.9 us
    dynamic_slice x32, local copies, waits for them, and re-layouts, place_shot(): where = starts[index] + DRIFT  20.8 us
    dynamic_update_slice x32, local copies, waits for them, and re-layouts, place_shot(): return lax.dynamic_update_slice_in_dim(buffer, current + piece, where, 1)  17.9 us
    all_to_all x1, waiting for transfers between devices, shards(): lax.all_to_all(far_traces, 'shot', split_axis=0, concat_axis=1, tiled=True)  15 us
    all_to_all x1, waiting for transfers between devices, shards(): lax.all_to_all(spectrum, 'shot', split_axis=2, concat_axis=1, tiled=True)  9.25 us
    all_to_all x1, starting transfers between devices, shards(): lax.all_to_all(spectrum, 'shot', split_axis=2, concat_axis=1, tiled=True)  7.03 us
  transfers between devices with their start and end apart: 5, of which 4 were waited for; matrix products, arithmetic and copies ran while one was open for 1% of the time, Pallas kernels for 0%

commit v1 on v0

v1 whole, which is shorter than its diff:
```python
import math

import jax
import jax.numpy as jnp
import ml_dtypes
import numpy as np
from jax import lax
from jax.experimental import pallas as pl
from jax.experimental.pallas import tpu as pltpu
from jax.sharding import PartitionSpec as P

SHOTS = 512
NT = 512
FREQS = 256
LANES = 128
PERIOD = 128
PARTS = 16
OWN = SHOTS // PARTS
HALF = OWN // 2
BLOCKS = NT // LANES
RIM = 6
PAYLOAD = OWN * (BLOCKS + 1) + 16
VMEM_LIMIT = 48 << 20


def wave(rows, columns, size):
    phases = np.outer(rows, columns) % size
    angles = phases.astype(np.float64) * (2.0 * math.pi / size)
    scale = 1.0 / math.sqrt(size)
    return np.cos(angles) * scale, np.sin(angles) * scale


def rounded(table):
    return np.ascontiguousarray(table).astype(np.float32).astype(ml_dtypes.bfloat16)


def time_tables():
    cosines, sines = wave(np.arange(NT), np.arange(FREQS), NT)
    forward = rounded(np.concatenate([cosines, -sines], axis=1))
    return forward, np.ascontiguousarray(forward.T)


def shot_tables():
    low = np.arange(SHOTS // 2)
    even, odd = np.arange(0, SHOTS, 2), np.arange(1, SHOTS, 2)
    pieces = [np.concatenate(wave(low, part, SHOTS), axis=1) for part in (even, odd)]
    inverse = np.concatenate(wave(np.arange(SHOTS), np.arange(SHOTS), SHOTS), axis=1)
    return rounded(np.stack(pieces)), rounded(inverse)


def swap_table():
    rows = np.arange(256)
    table = np.zeros((256, 256), np.float32)
    table[rows, (rows % 16) * 16 + rows // 16] = 1.0
    return table.astype(ml_dtypes.bfloat16)


def dot(a, b):
    return jnp.dot(a, b, preferred_element_type=jnp.float32)


def pack_kernel(fire_ref, delay_ref, estimate_ref, record_ref, swap_ref, out_ref):
    swap = swap_ref[...]
    estimate = estimate_ref[...].reshape(HALF, 2, PARTS, NT)
    for half in range(2):
        traces = estimate[:, half].reshape(HALF * PARTS, NT)
        turned = dot(swap, traces).astype(jnp.bfloat16).reshape(PARTS, HALF, NT)
        for block in range(BLOCKS):
            first = block * OWN + half * HALF
            out_ref[:, first : first + HALF, :] = turned[:, :, block * LANES : (block + 1) * LANES]
        pieces = [
            record_ref[:, (half * HALF + q) * LANES : (half * HALF + q + 1) * LANES]
            for q in range(HALF)
        ]
        rows = jnp.concatenate(pieces, axis=0).astype(jnp.bfloat16)
        first = BLOCKS * OWN + half * HALF
        out_ref[:, first : first + HALF, :] = (
            dot(swap, rows).astype(jnp.bfloat16).reshape(PARTS, HALF, LANES)
        )
    lane = lax.broadcasted_iota(jnp.int32, (16, LANES), 1)
    offsets = jnp.zeros((16, LANES), jnp.int32)
    for shot in range(OWN):
        offsets = jnp.where(lane == shot, fire_ref[shot] & (PERIOD - 1), offsets)
    first = (BLOCKS + 1) * OWN
    for part in range(PARTS):
        out_ref[part, first : first + 16, :] = (
            (offsets + delay_ref[part]).astype(jnp.float32).astype(jnp.bfloat16)
        )


def main_kernel(
    threshold_ref,
    data_ref,
    forward_ref,
    inverse_ref,
    split_ref,
    full_ref,
    out_ref,
    stack_ref,
    shrunk_ref,
    denoised_ref,
    offset_ref,
    placed_ref,
    difference_ref,
):
    half_shots = SHOTS // 2
    data = data_ref
    lane = lax.broadcasted_iota(jnp.int32, (OWN, LANES), 1)
    row = lax.broadcasted_iota(jnp.int32, (OWN, LANES), 0)
    first = (BLOCKS + 1) * OWN
    picked = []
    for part in range(PARTS):
        rows = data[part, first : first + 16, :].astype(jnp.float32)
        rows = jnp.concatenate([rows, rows], axis=0)
        picked.append(jnp.where(lane == row, rows, 0.0).astype(jnp.bfloat16))
    ones = jnp.ones((LANES, LANES), jnp.bfloat16)
    offset_ref[...] = dot(jnp.concatenate(picked, axis=0), ones).astype(jnp.int32)

    waves = []
    for half in range(2):
        traces = jnp.concatenate(
            [
                data[:, block * OWN + half * HALF : block * OWN + (half + 1) * HALF, :].reshape(
                    half_shots, LANES
                )
                for block in range(BLOCKS)
            ],
            axis=1,
        )
        spectrum = dot(traces, forward_ref[...]).astype(jnp.bfloat16)
        stack_ref[half, :half_shots, :] = spectrum
        stack_ref[half, half_shots:, :FREQS] = spectrum[:, FREQS:]
        stack_ref[half, half_shots:, FREQS:] = -spectrum[:, :FREQS]
        waves.append(dot(split_ref[half], stack_ref[half]))

    freq = lax.broadcasted_iota(jnp.int32, (1, FREQS), 1)
    weight = jnp.where(freq == 0, 1.0, 2.0).astype(jnp.float32)
    level = weight * threshold_ref[...]
    for half in range(2):
        fk = waves[0] + waves[1] if half == 0 else waves[0] - waves[1]
        real, imag = fk[:, :FREQS], fk[:, FREQS:]
        power = real * real + imag * imag + 1e-12
        factor = jnp.maximum(weight - level * lax.rsqrt(power), 0.0)
        real = (real * factor).astype(jnp.bfloat16)
        imag = (imag * factor).astype(jnp.bfloat16)
        here = slice(half * half_shots, (half + 1) * half_shots)
        there = slice(SHOTS + half * half_shots, SHOTS + (half + 1) * half_shots)
        shrunk_ref[here, :FREQS] = real
        shrunk_ref[here, FREQS:] = imag
        shrunk_ref[there, :FREQS] = -imag
        shrunk_ref[there, FREQS:] = real

    back = dot(full_ref[...], shrunk_ref[...]).astype(jnp.bfloat16)
    denoised_ref[...] = dot(back, inverse_ref[...])

    step = OWN
    zero = jnp.zeros((step, LANES), jnp.float32)

    def rotated(value, index):
        return jnp.take_along_axis(value, index, axis=1, mode="promise_in_bounds")

    for start in range(0, SHOTS, step):
        offset = offset_ref[start : start + step, :]
        index = (lane - offset) & (LANES - 1)
        near, far = lane >= offset, lane >= offset - LANES
        turned = [
            rotated(
                denoised_ref[start : start + step, block * LANES : (block + 1) * LANES], index
            )
            for block in range(BLOCKS)
        ]
        turned = [zero, zero] + turned + [zero, zero]
        for piece in range(RIM):
            placed_ref[piece, 8 + start : 8 + start + step, :] = jnp.where(
                near, turned[piece + 2], jnp.where(far, turned[piece + 1], turned[piece])
            )
    for piece in range(1, RIM):
        placed_ref[piece, 0:8, :] = placed_ref[piece, SHOTS : SHOTS + 8, :]

    for start in range(0, SHOTS, step):
        total = placed_ref[0, 8 + start : 8 + start + step, :]
        for piece in range(1, RIM):
            total = total + placed_ref[piece, 8 + start - piece : 8 + start - piece + step, :]
        record = data[start // step, BLOCKS * OWN : BLOCKS * OWN + step, :].astype(jnp.float32)
        difference_ref[start : start + step, :] = 0.5 * (record - total)
    difference_ref[SHOTS : SHOTS + 8, :] = difference_ref[0:8, :]

    for start in range(0, SHOTS, step):
        offset = offset_ref[start : start + step, :]
        index = (lane + offset) & (LANES - 1)
        near, far = lane >= offset, lane >= offset - LANES
        rows = [difference_ref[start + piece : start + piece + step, :] for piece in range(RIM)]
        rows[0] = jnp.where(near, rows[0], rows[4])
        rows[1] = jnp.where(far, rows[1], rows[5])
        turned = [rotated(rows[block], index) for block in range(BLOCKS)]
        reach = lane + offset
        one, two = reach >= LANES, reach >= 2 * LANES
        for block in range(BLOCKS):
            residual = jnp.where(
                two,
                turned[(block + 2) % BLOCKS],
                jnp.where(one, turned[(block + 1) % BLOCKS], turned[block]),
            )
            lanes = slice(block * LANES, (block + 1) * LANES)
            out_ref[start : start + step, lanes] = (
                denoised_ref[start : start + step, lanes] + residual
            ).astype(jnp.bfloat16)


def unpack_kernel(data_ref, swap_ref, out_ref):
    swap = swap_ref[...]
    for half in range(2):
        rows = data_ref[:, half * HALF : (half + 1) * HALF, :].reshape(PARTS * HALF, NT)
        out_ref[half * HALF : (half + 1) * HALF] = (
            dot(swap, rows).astype(jnp.bfloat16).reshape(HALF, PARTS, NT)
        )


def vmem():
    return pl.BlockSpec(memory_space=pltpu.VMEM)


def smem():
    return pl.BlockSpec(memory_space=pltpu.SMEM)


PARAMS = pltpu.CompilerParams(vmem_limit_bytes=VMEM_LIMIT)


def shards(estimate, record, fire_times, rcv_delay, threshold):
    forward, inverse = time_tables()
    split, full = shot_tables()
    swap = jnp.asarray(swap_table())
    packed = pl.pallas_call(
        pack_kernel,
        out_shape=jax.ShapeDtypeStruct((PARTS, PAYLOAD, LANES), jnp.bfloat16),
        in_specs=[smem(), smem(), vmem(), vmem(), vmem()],
        out_specs=vmem(),
        compiler_params=PARAMS,
        name="pack",
    )(fire_times, rcv_delay, estimate, record, swap)
    gathered = lax.all_to_all(packed, "shot", split_axis=0, concat_axis=0, tiled=True)
    updated = pl.pallas_call(
        main_kernel,
        out_shape=jax.ShapeDtypeStruct((SHOTS, NT), jnp.bfloat16),
        in_specs=[vmem()] * 6,
        out_specs=vmem(),
        scratch_shapes=[
            pltpu.VMEM((2, SHOTS, NT), jnp.bfloat16),
            pltpu.VMEM((2 * SHOTS, NT), jnp.bfloat16),
            pltpu.VMEM((SHOTS, NT), jnp.float32),
            pltpu.VMEM((SHOTS, LANES), jnp.int32),
            pltpu.VMEM((RIM, SHOTS + 8, LANES), jnp.float32),
            pltpu.VMEM((SHOTS + 8, LANES), jnp.float32),
        ],
        compiler_params=PARAMS,
        name="main",
    )(
        threshold.reshape(1, FREQS),
        gathered,
        jnp.asarray(forward),
        jnp.asarray(inverse),
        jnp.asarray(split),
        jnp.asarray(full),
    )
    returned = lax.all_to_all(
        updated.reshape(PARTS, OWN, NT), "shot", split_axis=0, concat_axis=0, tiled=True
    )
    return pl.pallas_call(
        unpack_kernel,
        out_shape=jax.ShapeDtypeStruct((OWN, PARTS, NT), jnp.bfloat16),
        in_specs=[vmem()] * 2,
        out_specs=vmem(),
        compiler_params=PARAMS,
        name="unpack",
    )(returned, swap)


def solution(mesh):
    in_specs = (P("shot", "rcv", None), P("rcv", "shot"), P("shot"), P("rcv"), P())
    out_specs = P("shot", "rcv", None)
    return jax.shard_map(shards, mesh=mesh, in_specs=in_specs, out_specs=out_specs, check_vma=False)
```

time: 302 us -> 44.8 us (0.15)
  local copies, waits for them, and re-layouts: 165 us -> 4.88 us
  loops' own time: 41.9 us -> 0 us
  matrix products: 37.7 us -> 0 us
  blocking collectives: 0 us -> 34.5 us
  waiting for transfers between devices: 28.7 us -> 0 us
  starting transfers between devices: 16.2 us -> 0 us
  other arithmetic: 10.1 us -> 0 us
  Pallas kernels: 0 us -> 5.16 us
    gather x224 -> x0, local copies, waits for them, and re-layouts: 121 us -> none
    another operation x4 -> x0, loops' own time: 41.9 us -> none  [the longest x1 40.9 us: shards(): lax.fori_loop(0, shot_count, place_shot, jnp.zeros((rcv_count, placed_len...]
    dot_general x10 -> x0, matrix products: 37.7 us -> none  [the longest x1 5.29 us: shards(): jnp.einsum('ks,srf->krf', sin_table, gathered[1], preferred_element_type=...]
    all_to_all x0 -> x2, blocking collectives: none -> 34.5 us  [the longest x1 20.6 us: shards(): lax.all_to_all(packed, 'shot', split_axis=0, concat_axis=0, tiled=True)]
    all_to_all x2 -> x0, waiting for transfers between devices: 24.3 us -> none  [the longest x1 15 us: shards(): lax.all_to_all(far_traces, 'shot', split_axis=0, concat_axis=1, tiled=True)]
    dynamic_slice x32 -> x0, local copies, waits for them, and re-layouts: 20.8 us -> none  [place_shot(): where = starts[index] + DRIFT]
    dynamic_update_slice x32 -> x0, local copies, waits for them, and re-layouts: 17.9 us -> none  [place_shot(): return lax.dynamic_update_slice_in_dim(buffer, current + piece, where, 1)]
    all_to_all x2 -> x0, starting transfers between devices: 10.7 us -> none  [the longest x1 7.03 us: shards(): lax.all_to_all(spectrum, 'shot', split_axis=2, concat_axis=1, tiled=True)]
  transfers between devices with their start and end apart: 5 -> 0, of which waited for: 4 -> 0; matrix products, arithmetic and copies ran while one was open for 1% -> 0% of each run, Pallas kernels for 0% -> 0%
where the time goes in v1:
time: 44.8 us; the launch traced here: 44.6 us
  blocking collectives  34.5 us (77%)
  Pallas kernels  5.16 us (12%)
  local copies, waits for them, and re-layouts  4.88 us (11%)
    all_to_all x1, blocking collectives, shards(): lax.all_to_all(packed, 'shot', split_axis=0, concat_axis=0, tiled=True)  20.6 us
    all_to_all x1, blocking collectives, shards(): lax.all_to_all(updated.reshape(PARTS, OWN, NT), 'shot', split_axis=0, con...  13.9 us
    unnamed x20, local copies, waits for them, and re-layouts  4.88 us
    pallas_call x1, Pallas kernels, shards(): pl.pallas_call(main_kernel, out_shape=jax.ShapeDtypeStruct((SHOTS, NT), j...  3.16 us
    pallas_call x1, Pallas kernels, shards(): pl.pallas_call(unpack_kernel, out_shape=jax.ShapeDtypeStruct((OWN, PARTS,...  1.09 us
    pallas_call x1, Pallas kernels, shards(): pl.pallas_call(pack_kernel, out_shape=jax.ShapeDtypeStruct((PARTS, PAYLOA...  0.91 us

profile of v1, /device:TPU:160, one launch (start us, length us, event | category | flops | bytes accessed | tf_op | source)
XLA Modules:
  0.0 44.6 jit_solution(9131936762122243030)
XLA Ops:
  0.0 0.0 copy-start.1
  0.0 1.0 %copy-done.1 = bf16[32,16,512]{2,1,0:T(8,128)(2,1)S(1)} copy-done((bf16[32,16,512]{2,1,0:T(8,128)(2,1)S(1)}, bf16[32,16,512]{2,1,0:T(8,128)(2,1)}, u32[]{:S(2)}) %copy-start.1) | copy-done | bytes 524312
  1.0 0.0 copy-start.5
  1.0 0.9 %copy-done.5 = bf16[256,256]{1,0:T(8,128)(2,1)S(1)} copy-done((bf16[256,256]{1,0:T(8,128)(2,1)S(1)}, bf16[256,256]{1,0:T(8,128)(2,1)}, u32[]{:S(2)}) %copy-start.5) | copy-done | bytes 131096
  1.9 0.0 copy-start.6
  1.9 0.9 %copy-done.6 = f32[16,4096]{1,0:T(8,128)S(1)} copy-done((f32[16,4096]{1,0:T(8,128)S(1)}, f32[16,4096]{1,0:T(8,128)}, u32[]{:S(2)}) %copy-start.6) | copy-done | bytes 262168
  2.9 0.0 copy-start.8
  2.9 0.7 %copy-done.8 = s32[32]{0:T(128)S(1)} copy-done((s32[32]{0:T(128)S(1)}, s32[32]{0:T(128)}, u32[]{:S(2)}) %copy-start.8) | copy-done | bytes 152
  3.6 0.0 copy-start.9
  3.6 0.7 %copy-done.9 = s32[16]{0:T(128)S(1)} copy-done((s32[16]{0:T(128)S(1)}, s32[16]{0:T(128)}, u32[]{:S(2)}) %copy-start.9) | copy-done | bytes 88
  4.2 0.0 copy-start.2
  4.2 0.0 copy-start.3
  4.2 0.0 copy-start.4
  4.2 0.9 %pack.1 = bf16[16,176,128]{2,1,0:T(8,128)(2,1)S(1)} custom-call(s32[32]{0:T(128)S(1)} %copy-done.8, s32[16]{0:T(128)S(1)} %copy-done.9, bf16[32,16,512]{2,1,0:T(8,128)(2,1)S(1)} %copy-done.1, f32[16,4096]{1,0:T(8,128)S(1)} %copy-done.6, bf16[256,256]{1,0:T(8,128)(2,1)S(1)} %copy-done.5), custom_call_target="tpu_custom_call" | custom-call | tf_op jit(solution)/shard_map/pack/pallas_call | solution.py:234
  5.1 0.0 copy-start
  5.1 20.6 %all_to_all.10.data_ref = bf16[16,176,128]{2,1,0:T(8,128)(2,1)S(1)} all-to-all(bf16[16,176,128]{2,1,0:T(8,128)(2,1)S(1)} %pack.1), channel_id=1, replica_groups=mesh['shot'=16,'rcv'=16] {'shot'}, dimensions={0} | all-to-all | bytes 1441792 | tf_op jit(solution)/shard_map/all_to_all | solution.py:242
  25.8 0.0 copy-start.7
  25.8 0.0 copy-done.2
  25.8 0.0 copy-done.3
  25.8 0.0 copy-done.4
  25.8 0.0 copy-done
  25.8 0.7 %copy-done.7 = f32[256]{0:T(256)S(1)} copy-done((f32[256]{0:T(256)S(1)}, f32[256]{0:T(256)}, u32[]{:S(2)}) %copy-start.7) | copy-done | bytes 1048
  26.4 3.2 %main.1 = bf16[512,512]{1,0:T(8,128)(2,1)S(1)} custom-call(f32[1,256]{1,0:T(1,128)S(1)} %bitcast.3, bf16[16,176,128]{2,1,0:T(8,128)(2,1)S(1)} %all_to_all.10.data_ref, bf16[512,512]{1,0:T(8,128)(2,1)S(1)} %copy-done.4, bf16[512,512]{1,0:T(8,128)(2,1)S(1)} %copy-done.3, bf16[2,256,512]{2,1,0:T(8,128)(2,1)S(1)} %copy-done.2, bf16[512,1024]{1,0:T(8,128)(2,1)S(1)} %copy-done), custom_call_target="tpu_custom_call" | custom-call | tf_op jit(solution)/shard_map/main/pallas_call | solution.py:243
  29.6 13.9 %all_to_all.11.data_ref = bf16[16,32,512]{2,1,0:T(8,128)(2,1)S(1)} all-to-all(bf16[16,32,512]{2,1,0:T(8,128)(2,1)S(1)} %bitcast.2), channel_id=1, replica_groups=mesh['shot'=16,'rcv'=16] {'shot'}, dimensions={0} | all-to-all | bytes 1048576 | tf_op jit(solution)/shard_map/all_to_all | solution.py:266
  43.5 1.1 %unpack.1 = bf16[32,16,512]{2,1,0:T(8,128)(2,1)} custom-call(bf16[16,32,512]{2,1,0:T(8,128)(2,1)S(1)} %all_to_all.11.data_ref, bf16[256,256]{1,0:T(8,128)(2,1)S(1)} %copy-done.5), custom_call_target="tpu_custom_call" | custom-call | tf_op jit(solution)/shard_map/unpack/pallas_call | solution.py:269
Async XLA Ops:
  0.0 1.0 %copy-start.1 = (bf16[32,16,512]{2,1,0:T(8,128)(2,1)S(1)}, bf16[32,16,512]{2,1,0:T(8,128)(2,1)}, u32[]{:S(2)}) copy-start(bf16[32,16,512]{2,1,0:T(8,128)(2,1)} %estimate_ref.1) | copy-start | bytes 1572868
  1.0 0.9 %copy-start.5 = (bf16[256,256]{1,0:T(8,128)(2,1)S(1)}, bf16[256,256]{1,0:T(8,128)(2,1)}, u32[]{:S(2)}) copy-start(bf16[256,256]{1,0:T(8,128)(2,1)} %constant.10.clone.swap_ref) | copy-start | bytes 393220
  1.9 0.9 %copy-start.6 = (f32[16,4096]{1,0:T(8,128)S(1)}, f32[16,4096]{1,0:T(8,128)}, u32[]{:S(2)}) copy-start(f32[16,4096]{1,0:T(8,128)} %record_ref.1) | copy-start | bytes 786436
  2.9 0.7 %copy-start.8 = (s32[32]{0:T(128)S(1)}, s32[32]{0:T(128)}, u32[]{:S(2)}) copy-start(s32[32]{0:T(128)} %fire_ref.1) | copy-start | bytes 388
  3.6 0.7 %copy-start.9 = (s32[16]{0:T(128)S(1)}, s32[16]{0:T(128)}, u32[]{:S(2)}) copy-start(s32[16]{0:T(128)} %delay_ref.1) | copy-start | bytes 196
  4.2 21.5 %copy-start.2 = (bf16[2,256,512]{2,1,0:T(8,128)(2,1)S(1)}, bf16[2,256,512]{2,1,0:T(8,128)(2,1)}, u32[]{:S(2)}) copy-start(bf16[2,256,512]{2,1,0:T(8,128)(2,1)} %constant.13.clone.split_ref) | copy-start | bytes 1572868
  4.2 21.5 %copy-start.3 = (bf16[512,512]{1,0:T(8,128)(2,1)S(1)}, bf16[512,512]{1,0:T(8,128)(2,1)}, u32[]{:S(2)}) copy-start(bf16[512,512]{1,0:T(8,128)(2,1)} %constant.12.clone.inverse_ref) | copy-start | bytes 1572868
  4.2 21.5 %copy-start.4 = (bf16[512,512]{1,0:T(8,128)(2,1)S(1)}, bf16[512,512]{1,0:T(8,128)(2,1)}, u32[]{:S(2)}) copy-start(bf16[512,512]{1,0:T(8,128)(2,1)} %constant.11.clone.forward_ref) | copy-start | bytes 1572868
  5.1 20.6 %copy-start = (bf16[512,1024]{1,0:T(8,128)(2,1)S(1)}, bf16[512,1024]{1,0:T(8,128)(2,1)}, u32[]{:S(2)}) copy-start(bf16[512,1024]{1,0:T(8,128)(2,1)} %constant.14.clone.full_ref) | copy-start | bytes 3145732
  25.8 0.7 %copy-start.7 = (f32[256]{0:T(256)S(1)}, f32[256]{0:T(256)}, u32[]{:S(2)}) copy-start(f32[256]{0:T(256)} %param.14) | copy-start | bytes 3076

commit v2 on v1

--- a/solution.py
+++ b/solution.py
@@ -19,7 +19,7 @@
 HALF = OWN // 2
 BLOCKS = NT // LANES
 RIM = 6
-PAYLOAD = OWN * (BLOCKS + 1) + 16
+PAYLOAD = OWN * (BLOCKS + 1) + 8
 VMEM_LIMIT = 48 << 20
 
 
@@ -48,26 +48,66 @@
     return rounded(np.stack(pieces)), rounded(inverse)
 
 
-def swap_table():
-    rows = np.arange(256)
-    table = np.zeros((256, 256), np.float32)
-    table[rows, (rows % 16) * 16 + rows // 16] = 1.0
-    return table.astype(ml_dtypes.bfloat16)
-
-
 def dot(a, b):
     return jnp.dot(a, b, preferred_element_type=jnp.float32)
 
 
-def pack_kernel(fire_ref, delay_ref, estimate_ref, record_ref, swap_ref, out_ref):
-    swap = swap_ref[...]
-    estimate = estimate_ref[...].reshape(HALF, 2, PARTS, NT)
-    for half in range(2):
-        traces = estimate[:, half].reshape(HALF * PARTS, NT)
-        turned = dot(swap, traces).astype(jnp.bfloat16).reshape(PARTS, HALF, NT)
+def swap_table():
+    row = lax.broadcasted_iota(jnp.int32, (256, 256), 0)
+    column = lax.broadcasted_iota(jnp.int32, (256, 256), 1)
+    source = (row & 15) * 16 + (row >> 4)
+    return jnp.where(column == source, 1.0, 0.0).astype(jnp.bfloat16)
+
+
+def pack_kernel(
+    fire_hbm,
+    delay_hbm,
+    estimate_hbm,
+    record_hbm,
+    out_ref,
+    fire_ref,
+    delay_ref,
+    estimate_ref,
+    record_ref,
+    small_sems,
+    trace_sems,
+    record_sem,
+):
+    halves = []
+    for half in range(2):
+        halves.append(
+            pltpu.make_async_copy(
+                estimate_hbm.at[:, half], estimate_ref.at[half], trace_sems.at[half]
+            )
+        )
+        halves[-1].start()
+    whole = pltpu.make_async_copy(record_hbm, record_ref, record_sem)
+    whole.start()
+    fires = pltpu.make_async_copy(fire_hbm, fire_ref, small_sems.at[0])
+    delays = pltpu.make_async_copy(delay_hbm, delay_ref, small_sems.at[1])
+    fires.start()
+    delays.start()
+    swap = swap_table()
+    lane = lax.broadcasted_iota(jnp.int32, (8, LANES), 1)
+    offsets = jnp.zeros((8, LANES), jnp.int32)
+    fires.wait()
+    delays.wait()
+    for shot in range(OWN):
+        offsets = jnp.where(lane == shot, fire_ref[shot] & (PERIOD - 1), offsets)
+    first = (BLOCKS + 1) * OWN
+    for part in range(PARTS):
+        out_ref[part, first : first + 8, :] = (
+            (offsets + delay_ref[part]).astype(jnp.float32).astype(jnp.bfloat16)
+        )
+    for half in range(2):
+        halves[half].wait()
+        turned = dot(swap, estimate_ref[half].reshape(HALF * PARTS, NT)).astype(jnp.bfloat16)
+        turned = turned.reshape(PARTS, HALF, NT)
         for block in range(BLOCKS):
             first = block * OWN + half * HALF
             out_ref[:, first : first + HALF, :] = turned[:, :, block * LANES : (block + 1) * LANES]
+    whole.wait()
+    for half in range(2):
         pieces = [
             record_ref[:, (half * HALF + q) * LANES : (half * HALF + q + 1) * LANES]
             for q in range(HALF)
@@ -77,19 +117,10 @@
         out_ref[:, first : first + HALF, :] = (
             dot(swap, rows).astype(jnp.bfloat16).reshape(PARTS, HALF, LANES)
         )
-    lane = lax.broadcasted_iota(jnp.int32, (16, LANES), 1)
-    offsets = jnp.zeros((16, LANES), jnp.int32)
-    for shot in range(OWN):
-        offsets = jnp.where(lane == shot, fire_ref[shot] & (PERIOD - 1), offsets)
-    first = (BLOCKS + 1) * OWN
-    for part in range(PARTS):
-        out_ref[part, first : first + 16, :] = (
-            (offsets + delay_ref[part]).astype(jnp.float32).astype(jnp.bfloat16)
-        )
 
 
 def main_kernel(
-    threshold_ref,
+    threshold_hbm,
     data_ref,
     forward_ref,
     inverse_ref,
@@ -102,7 +133,11 @@
     offset_ref,
     placed_ref,
     difference_ref,
+    threshold_ref,
+    threshold_sem,
 ):
+    fetch = pltpu.make_async_copy(threshold_hbm, threshold_ref, threshold_sem)
+    fetch.start()
     half_shots = SHOTS // 2
     data = data_ref
     lane = lax.broadcasted_iota(jnp.int32, (OWN, LANES), 1)
@@ -110,8 +145,8 @@
     first = (BLOCKS + 1) * OWN
     picked = []
     for part in range(PARTS):
-        rows = data[part, first : first + 16, :].astype(jnp.float32)
-        rows = jnp.concatenate([rows, rows], axis=0)
+        rows = data[part, first : first + 8, :].astype(jnp.float32)
+        rows = jnp.concatenate([rows] * 4, axis=0)
         picked.append(jnp.where(lane == row, rows, 0.0).astype(jnp.bfloat16))
     ones = jnp.ones((LANES, LANES), jnp.bfloat16)
     offset_ref[...] = dot(jnp.concatenate(picked, axis=0), ones).astype(jnp.int32)
@@ -135,6 +170,7 @@
 
     freq = lax.broadcasted_iota(jnp.int32, (1, FREQS), 1)
     weight = jnp.where(freq == 0, 1.0, 2.0).astype(jnp.float32)
+    fetch.wait()
     level = weight * threshold_ref[...]
     for half in range(2):
         fk = waves[0] + waves[1] if half == 0 else waves[0] - waves[1]
@@ -207,21 +243,39 @@
             ).astype(jnp.bfloat16)
 
 
-def unpack_kernel(data_ref, swap_ref, out_ref):
-    swap = swap_ref[...]
-    for half in range(2):
-        rows = data_ref[:, half * HALF : (half + 1) * HALF, :].reshape(PARTS * HALF, NT)
-        out_ref[half * HALF : (half + 1) * HALF] = (
-            dot(swap, rows).astype(jnp.bfloat16).reshape(HALF, PARTS, NT)
-        )
+def unpack_kernel(data_ref, out_hbm, out_ref, sems):
+    swap = swap_table()
+    width = NT // 2
+    copies = []
+    for half in range(2):
+        shots = slice(half * HALF, (half + 1) * HALF)
+        for side in range(2):
+            lanes = slice(side * width, (side + 1) * width)
+            rows = data_ref[:, shots, lanes].reshape(PARTS * HALF, width)
+            out_ref[shots, :, lanes] = (
+                dot(swap, rows).astype(jnp.bfloat16).reshape(HALF, PARTS, width)
+            )
+            place = (pl.ds(half * HALF, HALF), slice(None), pl.ds(side * width, width))
+            copies.append(
+                pltpu.make_async_copy(
+                    out_ref.at[place], out_hbm.at[place], sems.at[2 * half + side]
+                )
+            )
+            copies[-1].start()
+    for copy in copies:
+        copy.wait()
 
 
 def vmem():
     return pl.BlockSpec(memory_space=pltpu.VMEM)
 
 
-def smem():
-    return pl.BlockSpec(memory_space=pltpu.SMEM)
+def hbm():
+    return pl.BlockSpec(memory_space=pltpu.HBM)
+
+
+def kept(value):
+    return pltpu.with_memory_space_constraint(value, pltpu.HBM)
 
 
 PARAMS = pltpu.CompilerParams(vmem_limit_bytes=VMEM_LIMIT)
@@ -230,20 +284,33 @@
 def shards(estimate, record, fire_times, rcv_delay, threshold):
     forward, inverse = time_tables()
     split, full = shot_tables()
-    swap = jnp.asarray(swap_table())
     packed = pl.pallas_call(
         pack_kernel,
         out_shape=jax.ShapeDtypeStruct((PARTS, PAYLOAD, LANES), jnp.bfloat16),
-        in_specs=[smem(), smem(), vmem(), vmem(), vmem()],
+        in_specs=[hbm()] * 4,
         out_specs=vmem(),
+        scratch_shapes=[
+            pltpu.SMEM((OWN,), jnp.int32),
+            pltpu.SMEM((PARTS,), jnp.int32),
+            pltpu.VMEM((2, HALF, PARTS, NT), jnp.bfloat16),
+            pltpu.VMEM((PARTS, OWN * LANES), jnp.float32),
+            pltpu.SemaphoreType.DMA((2,)),
+            pltpu.SemaphoreType.DMA((2,)),
+            pltpu.SemaphoreType.DMA,
+        ],
         compiler_params=PARAMS,
         name="pack",
-    )(fire_times, rcv_delay, estimate, record, swap)
+    )(
+        kept(fire_times),
+        kept(rcv_delay),
+        kept(estimate.reshape(HALF, 2, PARTS, NT)),
+        kept(record),
+    )
     gathered = lax.all_to_all(packed, "shot", split_axis=0, concat_axis=0, tiled=True)
     updated = pl.pallas_call(
         main_kernel,
         out_shape=jax.ShapeDtypeStruct((SHOTS, NT), jnp.bfloat16),
-        in_specs=[vmem()] * 6,
+        in_specs=[hbm()] + [vmem()] * 5,
         out_specs=vmem(),
         scratch_shapes=[
             pltpu.VMEM((2, SHOTS, NT), jnp.bfloat16),
@@ -252,11 +319,13 @@
             pltpu.VMEM((SHOTS, LANES), jnp.int32),
             pltpu.VMEM((RIM, SHOTS + 8, LANES), jnp.float32),
             pltpu.VMEM((SHOTS + 8, LANES), jnp.float32),
+            pltpu.VMEM((1, FREQS), jnp.float32),
+            pltpu.SemaphoreType.DMA,
         ],
         compiler_params=PARAMS,
         name="main",
     )(
-        threshold.reshape(1, FREQS),
+        kept(threshold.reshape(1, FREQS)),
         gathered,
         jnp.asarray(forward),
         jnp.asarray(inverse),
@@ -269,11 +338,15 @@
     return pl.pallas_call(
         unpack_kernel,
         out_shape=jax.ShapeDtypeStruct((OWN, PARTS, NT), jnp.bfloat16),
-        in_specs=[vmem()] * 2,
-        out_specs=vmem(),
+        in_specs=[vmem()],
+        out_specs=hbm(),
+        scratch_shapes=[
+            pltpu.VMEM((OWN, PARTS, NT), jnp.bfloat16),
+            pltpu.SemaphoreType.DMA((4,)),
+        ],
         compiler_params=PARAMS,
         name="unpack",
-    )(returned, swap)
+    )(returned)
 
 
 def solution(mesh):

time: 44.8 us -> 40.1 us (0.90)
  local copies, waits for them, and re-layouts: 4.88 us -> 0.02 us
  Pallas kernels: 5.16 us -> 6.13 us
  blocking collectives: 34.5 us -> 33.7 us
    unnamed x20 -> x8, local copies, waits for them, and re-layouts: 4.88 us -> 0.02 us
    pallas_call x1, Pallas kernels: 0.91 us -> 1.8 us  [shards(): pl.pallas_call(pack_kernel, out_shape=jax.ShapeDtypeStruct((PARTS, PAYLOA...]
where the time goes in v2:
time: 40.1 us; the launch traced here: 39.9 us
  blocking collectives  33.7 us (84%)
  Pallas kernels  6.13 us (15%)
    all_to_all x1, blocking collectives, shards(): lax.all_to_all(packed, 'shot', split_axis=0, concat_axis=0, tiled=True)  20.3 us
    all_to_all x1, blocking collectives, shards(): lax.all_to_all(updated.reshape(PARTS, OWN, NT), 'shot', split_axis=0, con...  13.5 us
    pallas_call x1, Pallas kernels, shards(): pl.pallas_call(main_kernel, out_shape=jax.ShapeDtypeStruct((SHOTS, NT), j...  3.28 us
    pallas_call x1, Pallas kernels, shards(): pl.pallas_call(pack_kernel, out_shape=jax.ShapeDtypeStruct((PARTS, PAYLOA...  1.8 us
    pallas_call x1, Pallas kernels, shards(): pl.pallas_call(unpack_kernel, out_shape=jax.ShapeDtypeStruct((OWN, PARTS,...  1.05 us

profile of v2, /device:TPU:160, one launch (start us, length us, event | category | flops | bytes accessed | tf_op | source)
XLA Modules:
  0.0 39.9 jit_solution(5463288213929914322)
XLA Ops:
  0.0 0.0 copy-start.1
  0.0 0.0 copy-start.2
  0.0 0.0 copy-start.3
  0.0 1.8 %pack.1 = bf16[16,168,128]{2,1,0:T(8,128)(2,1)S(1)} custom-call(s32[32]{0:T(128)} %fire_hbm.1, s32[16]{0:T(128)} %delay_hbm.1, bf16[16,2,16,512]{3,2,1,0:T(8,128)(2,1)} %bitcast.4, f32[16,4096]{1,0:T(8,128)} %record_hbm.1), custom_call_target="tpu_custom_call" | custom-call | tf_op jit(solution)/shard_map/pack/pallas_call | solution.py:287
  1.8 0.0 copy-start
  1.8 20.3 %all_to_all.10.data_ref = bf16[16,168,128]{2,1,0:T(8,128)(2,1)S(1)} all-to-all(bf16[16,168,128]{2,1,0:T(8,128)(2,1)S(1)} %pack.1), channel_id=1, replica_groups=mesh['shot'=16,'rcv'=16] {'shot'}, dimensions={0} | all-to-all | bytes 1376256 | tf_op jit(solution)/shard_map/all_to_all | solution.py:309
  22.1 0.0 copy-done.1
  22.1 0.0 copy-done.2
  22.1 0.0 copy-done.3
  22.1 0.0 copy-done
  22.1 3.3 %main.1 = bf16[512,512]{1,0:T(8,128)(2,1)S(1)} custom-call(f32[1,256]{1,0:T(1,128)} %bitcast.5, bf16[16,168,128]{2,1,0:T(8,128)(2,1)S(1)} %all_to_all.10.data_ref, bf16[512,512]{1,0:T(8,128)(2,1)S(1)} %copy-done.3, bf16[512,512]{1,0:T(8,128)(2,1)S(1)} %copy-done.2, bf16[2,256,512]{2,1,0:T(8,128)(2,1)S(1)} %copy-done.1, bf16[512,1024]{1,0:T(8,128)(2,1)S(1)} %copy-done), custom_call_target="tpu_custom_call" | custom-call | tf_op jit(solution)/shard_map/main/pallas_call | solution.py:310
  25.4 13.5 %all_to_all.11.data_ref = bf16[16,32,512]{2,1,0:T(8,128)(2,1)S(1)} all-to-all(bf16[16,32,512]{2,1,0:T(8,128)(2,1)S(1)} %bitcast.3), channel_id=1, replica_groups=mesh['shot'=16,'rcv'=16] {'shot'}, dimensions={0} | all-to-all | bytes 1048576 | tf_op jit(solution)/shard_map/all_to_all | solution.py:335
  38.9 1.1 %unpack.1 = bf16[32,16,512]{2,1,0:T(8,128)(2,1)} custom-call(bf16[16,32,512]{2,1,0:T(8,128)(2,1)S(1)} %all_to_all.11.data_ref), custom_call_target="tpu_custom_call" | custom-call | tf_op jit(solution)/shard_map/unpack/pallas_call | solution.py:338
Async XLA Ops:
  0.0 22.1 %copy-start.1 = (bf16[2,256,512]{2,1,0:T(8,128)(2,1)S(1)}, bf16[2,256,512]{2,1,0:T(8,128)(2,1)}, u32[]{:S(2)}) copy-start(bf16[2,256,512]{2,1,0:T(8,128)(2,1)} %constant.10.clone.split_ref) | copy-start | bytes 1572868
  0.0 22.1 %copy-start.2 = (bf16[512,512]{1,0:T(8,128)(2,1)S(1)}, bf16[512,512]{1,0:T(8,128)(2,1)}, u32[]{:S(2)}) copy-start(bf16[512,512]{1,0:T(8,128)(2,1)} %constant.9.clone.inverse_ref) | copy-start | bytes 1572868
  0.0 22.1 %copy-start.3 = (bf16[512,512]{1,0:T(8,128)(2,1)S(1)}, bf16[512,512]{1,0:T(8,128)(2,1)}, u32[]{:S(2)}) copy-start(bf16[512,512]{1,0:T(8,128)(2,1)} %constant.8.clone.forward_ref) | copy-start | bytes 1572868
  1.8 20.3 %copy-start = (bf16[512,1024]{1,0:T(8,128)(2,1)S(1)}, bf16[512,1024]{1,0:T(8,128)(2,1)}, u32[]{:S(2)}) copy-start(bf16[512,1024]{1,0:T(8,128)(2,1)} %constant.11.clone.full_ref) | copy-start | bytes 3145732

commit v3 on v2

v3 whole, which is shorter than its diff:
```python
import math

import jax
import jax.numpy as jnp
import ml_dtypes
import numpy as np
from jax import lax
from jax.experimental import pallas as pl
from jax.experimental.pallas import tpu as pltpu
from jax.sharding import PartitionSpec as P

SHOTS = 512
NT = 512
FREQS = 256
LANES = 128
PERIOD = 128
PARTS = 16
OWN = SHOTS // PARTS
HALF = OWN // 2
BLOCKS = NT // LANES
RIM = 6
PAYLOAD = OWN * BLOCKS + 8
CHUNKS = 2
VMEM_LIMIT = 24 << 20


def wave(rows, columns, size):
    phases = np.outer(rows, columns) % size
    angles = phases.astype(np.float64) * (2.0 * math.pi / size)
    scale = 1.0 / math.sqrt(size)
    return np.cos(angles) * scale, np.sin(angles) * scale


def rounded(table):
    return np.ascontiguousarray(table).astype(np.float32).astype(ml_dtypes.bfloat16)


def tables():
    low = np.arange(SHOTS // 2)
    even, odd = np.arange(0, SHOTS, 2), np.arange(1, SHOTS, 2)
    pieces = [np.concatenate(wave(low, part, SHOTS), axis=1) for part in (even, odd)]
    inverse = np.concatenate(wave(np.arange(SHOTS), np.arange(SHOTS), SHOTS), axis=1)
    return rounded(np.stack(pieces)), rounded(inverse)


def dot(a, b):
    return jnp.dot(a, b, preferred_element_type=jnp.float32)


def swap_table():
    row = lax.broadcasted_iota(jnp.int32, (256, 256), 0)
    column = lax.broadcasted_iota(jnp.int32, (256, 256), 1)
    source = (row & 15) * 16 + (row >> 4)
    return jnp.where(column == source, 1.0, 0.0).astype(jnp.bfloat16)


def pack_kernel(
    fire_hbm,
    delay_hbm,
    estimate_hbm,
    record_hbm,
    out_ref,
    fire_ref,
    delay_ref,
    estimate_ref,
    record_ref,
    small_sems,
    in_sems,
):
    pieces = [(half, 0) for half in range(2)]
    width = NT
    arrivals = []
    for at, (half, side) in enumerate(pieces):
        arrivals.append(
            pltpu.make_async_copy(
                estimate_hbm.at[:, half],
                estimate_ref.at[half],
                in_sems.at[at],
            )
        )
    fires = pltpu.make_async_copy(fire_hbm, fire_ref, small_sems.at[0])
    delays = pltpu.make_async_copy(delay_hbm, delay_ref, small_sems.at[1])
    heads = pltpu.make_async_copy(
        record_hbm.at[:, pl.ds(0, RIM * LANES)], record_ref, small_sems.at[2]
    )
    arrivals[0].start()
    fires.start()
    delays.start()
    heads.start()
    for arrival in arrivals[1:]:
        arrival.start()
    swap = swap_table()
    def turn(at):
        half, side = pieces[at]
        arrivals[at].wait()
        traces = estimate_ref[half]
        turned = dot(swap, traces.reshape(HALF * PARTS, width)).astype(jnp.bfloat16)
        turned = turned.reshape(PARTS, HALF, width)
        for block in range(4):
            first = (4 * half + block) * HALF
            out_ref[:, first : first + HALF, :] = turned[:, :, block * LANES : (block + 1) * LANES]

    turn(0)
    lane = lax.broadcasted_iota(jnp.int32, (8, LANES), 1)
    row = lax.broadcasted_iota(jnp.int32, (8, LANES), 0)
    offsets = jnp.zeros((8, LANES), jnp.int32)
    fires.wait()
    delays.wait()
    for shot in range(OWN):
        offsets = jnp.where(lane == shot, fire_ref[shot] & (PERIOD - 1), offsets)
    heads.wait()
    for part in range(PARTS):
        rows = (offsets + delay_ref[part]).astype(jnp.float32)
        for piece in range(RIM):
            head = record_ref[part : part + 1, piece * LANES : (piece + 1) * LANES]
            rows = jnp.where(row == piece, jnp.broadcast_to(head, (8, LANES)), rows)
        out_ref[part, BLOCKS * OWN : BLOCKS * OWN + 8, :] = rows.astype(jnp.bfloat16)
    turn(1)


def rotated(value, index):
    return jnp.take_along_axis(value, index, axis=1, mode="promise_in_bounds")


def read_windows(rows, offset, lane):
    near, far = lane >= offset, lane >= offset - LANES
    reach = lane + offset
    one, two = reach >= LANES, reach >= 2 * LANES
    rows = [jnp.where(near, rows[0], rows[4]), jnp.where(far, rows[1], rows[5]), *rows[2:4]]
    turned = [rotated(row, reach & (LANES - 1)) for row in rows]
    return [
        jnp.where(
            two,
            turned[(block + 2) % BLOCKS],
            jnp.where(one, turned[(block + 1) % BLOCKS], turned[block]),
        )
        for block in range(BLOCKS)
    ]


def main_kernel(
    threshold_hbm,
    fire_hbm,
    delay_hbm,
    record_hbm,
    data_ref,
    split_ref,
    full_ref,
    out_ref,
    window_ref,
    stack_ref,
    shrunk_ref,
    denoised_ref,
    offset_ref,
    placed_ref,
    difference_ref,
    threshold_ref,
    fire_ref,
    delay_ref,
    record_ref,
    sems,
):
    pairs = [
        (threshold_hbm, threshold_ref),
        (fire_hbm, fire_ref),
        (delay_hbm, delay_ref),
        (record_hbm, record_ref),
    ]
    fetches = [
        pltpu.make_async_copy(source, target, sems.at[at])
        for at, (source, target) in enumerate(pairs)
    ]
    for fetch in fetches:
        fetch.start()
    half_shots = SHOTS // 2
    data = data_ref
    lane = lax.broadcasted_iota(jnp.int32, (OWN, LANES), 1)
    row = lax.broadcasted_iota(jnp.int32, (OWN, LANES), 0)

    waves = []
    for half in range(2):
        traces = jnp.concatenate(
            [
                data[:, first : first + HALF, :].reshape(half_shots, LANES)
                for first in range(half * BLOCKS * HALF, (half + 1) * BLOCKS * HALF, HALF)
            ],
            axis=1,
        )
        real = dot(traces, full_ref[:, :FREQS]).astype(jnp.bfloat16)
        imag = (-dot(traces, full_ref[:, SHOTS : SHOTS + FREQS])).astype(jnp.bfloat16)
        stack_ref[half, :half_shots, :FREQS] = real
        stack_ref[half, :half_shots, FREQS:] = imag
        stack_ref[half, half_shots:, :FREQS] = imag
        stack_ref[half, half_shots:, FREQS:] = -real
        waves.append(dot(split_ref[half], stack_ref[half]))

    first = BLOCKS * OWN
    picked = []
    for part in range(PARTS):
        rows = data[part, first : first + 8, :].astype(jnp.float32)
        rows = jnp.broadcast_to(rows[7:8, :], (OWN, LANES))
        picked.append(jnp.where(lane == row, rows, 0.0).astype(jnp.bfloat16))
    ones = jnp.ones((LANES, LANES), jnp.bfloat16)
    offset_ref[...] = dot(jnp.concatenate(picked, axis=0), ones).astype(jnp.int32)

    for fetch in fetches:
        fetch.wait()
    freq = lax.broadcasted_iota(jnp.int32, (1, FREQS), 1)
    weight = jnp.where(freq == 0, 1.0, 2.0).astype(jnp.float32)
    level = weight * threshold_ref[...]
    for half in range(2):
        fk = waves[0] + waves[1] if half == 0 else waves[0] - waves[1]
        real, imag = fk[:, :FREQS], fk[:, FREQS:]
        power = real * real + imag * imag + 1e-12
        factor = jnp.maximum(weight - level * lax.rsqrt(power), 0.0)
        less = (-imag * factor).astype(jnp.bfloat16)
        real = (real * factor).astype(jnp.bfloat16)
        here = slice(half * half_shots, (half + 1) * half_shots)
        there = slice(SHOTS + half * half_shots, SHOTS + (half + 1) * half_shots)
        shrunk_ref[here, :FREQS] = real
        shrunk_ref[there, :FREQS] = less
        shrunk_ref[here, FREQS:] = less
        shrunk_ref[there, FREQS:] = -real

    wide = lax.broadcasted_iota(jnp.int32, (PARTS, LANES), 1)
    which = lax.broadcasted_iota(jnp.int32, (PARTS, LANES), 0)
    delay = jnp.zeros((PARTS, LANES), jnp.int32)
    for part in range(PARTS):
        delay = jnp.where(which == part, delay_ref[part], delay)

    def record_window(shot):
        rows = [
            record_ref[:, piece * LANES : (piece + 1) * LANES]
            if RIM <= piece < OWN
            else jnp.zeros((PARTS, LANES), jnp.float32)
            for piece in range(shot, shot + RIM)
        ]
        offset = delay + (fire_ref[shot] & (PERIOD - 1))
        for block, value in enumerate(read_windows(rows, offset, wide)):
            window_ref[shot, :, block * LANES : (block + 1) * LANES] = 0.5 * value

    step = OWN
    zero = jnp.zeros((step, LANES), jnp.float32)

    def place(start):
        offset = offset_ref[start : start + step, :]
        index = (lane - offset) & (LANES - 1)
        near, far = lane >= offset, lane >= offset - LANES
        turned = [
            rotated(
                denoised_ref[start : start + step, block * LANES : (block + 1) * LANES], index
            )
            for block in range(BLOCKS)
        ]
        turned = [zero, zero] + turned + [zero, zero]
        for piece in range(RIM):
            placed_ref[piece, 8 + start : 8 + start + step, :] = jnp.where(
                near, turned[piece + 2], jnp.where(far, turned[piece + 1], turned[piece])
            )

    def subtract(start):
        total = placed_ref[0, 8 + start : 8 + start + step, :]
        for piece in range(1, RIM):
            total = total + placed_ref[piece, 8 + start - piece : 8 + start - piece + step, :]
        difference_ref[start : start + step, :] = -0.5 * total
        heads = data[start // step, BLOCKS * OWN : BLOCKS * OWN + 8, :].astype(jnp.float32)
        heads = jnp.where(row[:8] < RIM, 0.5 * heads, 0.0)
        difference_ref[start : start + 8, :] = difference_ref[start : start + 8, :] + heads

    def finish(start):
        offset = offset_ref[start : start + step, :]
        rows = [difference_ref[start + piece : start + piece + step, :] for piece in range(RIM)]
        for block, value in enumerate(read_windows(rows, offset, lane)):
            lanes = slice(block * LANES, (block + 1) * LANES)
            out_ref[start : start + step, lanes] = (
                denoised_ref[start : start + step, lanes] + value
            ).astype(jnp.bfloat16)

    inverse = jnp.concatenate([full_ref[:FREQS, :SHOTS], full_ref[:FREQS, SHOTS:]], axis=0)
    part_shots = SHOTS // CHUNKS
    for part in range(CHUNKS):
        shots = slice(part * part_shots, (part + 1) * part_shots)
        back = dot(full_ref[shots, :], shrunk_ref[...]).astype(jnp.bfloat16)
        denoised_ref[shots, :] = dot(back, inverse)
        for shot in range(part * OWN // CHUNKS, (part + 1) * OWN // CHUNKS):
            record_window(shot)
        for start in range(part * part_shots, (part + 1) * part_shots, step):
            place(start)
    for piece in range(1, RIM):
        placed_ref[piece, 0:8, :] = placed_ref[piece, SHOTS : SHOTS + 8, :]
    for start in range(0, SHOTS, step):
        subtract(start)
    difference_ref[SHOTS : SHOTS + 8, :] = difference_ref[0:8, :]
    for start in range(0, SHOTS, step):
        finish(start)


def unpack_kernel(data_ref, window_ref, out_hbm, out_ref, sems):
    swap = swap_table()
    width = NT // 2
    copies = []
    for half in range(2):
        shots = slice(half * HALF, (half + 1) * HALF)
        for side in range(2):
            lanes = slice(side * width, (side + 1) * width)
            rows = data_ref[:, shots, lanes].reshape(PARTS * HALF, width)
            out_ref[shots, :, lanes] = (
                dot(swap, rows).reshape(HALF, PARTS, width) + window_ref[shots, :, lanes]
            ).astype(jnp.bfloat16)
            place = (pl.ds(half * HALF, HALF), slice(None), pl.ds(side * width, width))
            copies.append(
                pltpu.make_async_copy(
                    out_ref.at[place], out_hbm.at[place], sems.at[2 * half + side]
                )
            )
            copies[-1].start()
    for copy in copies:
        copy.wait()


def vmem():
    return pl.BlockSpec(memory_space=pltpu.VMEM)


def hbm():
    return pl.BlockSpec(memory_space=pltpu.HBM)


def kept(value):
    return pltpu.with_memory_space_constraint(value, pltpu.HBM)


PARAMS = pltpu.CompilerParams(vmem_limit_bytes=VMEM_LIMIT)


def shards(estimate, record, fire_times, rcv_delay, threshold):
    packed = pl.pallas_call(
        pack_kernel,
        out_shape=jax.ShapeDtypeStruct((PARTS, PAYLOAD, LANES), jnp.bfloat16),
        in_specs=[hbm()] * 4,
        out_specs=vmem(),
        scratch_shapes=[
            pltpu.SMEM((OWN,), jnp.int32),
            pltpu.SMEM((PARTS,), jnp.int32),
            pltpu.VMEM((2, HALF, PARTS, NT), jnp.bfloat16),
            pltpu.VMEM((PARTS, RIM * LANES), jnp.float32),
            pltpu.SemaphoreType.DMA((3,)),
            pltpu.SemaphoreType.DMA((2,)),
        ],
        compiler_params=PARAMS,
        name="pack",
    )(
        kept(fire_times),
        kept(rcv_delay),
        kept(estimate.reshape(HALF, 2, PARTS, NT)),
        kept(record),
    )
    gathered = lax.all_to_all(packed, "shot", split_axis=0, concat_axis=0, tiled=True)
    split, full = (jnp.asarray(table) for table in tables())
    updated, window = pl.pallas_call(
        main_kernel,
        out_shape=[
            jax.ShapeDtypeStruct((SHOTS, NT), jnp.bfloat16),
            jax.ShapeDtypeStruct((OWN, PARTS, NT), jnp.float32),
        ],
        in_specs=[hbm()] * 4 + [vmem()] * 3,
        out_specs=[vmem()] * 2,
        scratch_shapes=[
            pltpu.VMEM((2, SHOTS, NT), jnp.bfloat16),
            pltpu.VMEM((2 * SHOTS, NT), jnp.bfloat16),
            pltpu.VMEM((SHOTS, NT), jnp.float32),
            pltpu.VMEM((SHOTS, LANES), jnp.int32),
            pltpu.VMEM((RIM, SHOTS + 8, LANES), jnp.float32),
            pltpu.VMEM((SHOTS + 8, LANES), jnp.float32),
            pltpu.VMEM((1, FREQS), jnp.float32),
            pltpu.SMEM((OWN,), jnp.int32),
            pltpu.SMEM((PARTS,), jnp.int32),
            pltpu.VMEM((PARTS, OWN * LANES), jnp.float32),
            pltpu.SemaphoreType.DMA((4,)),
        ],
        compiler_params=PARAMS,
        name="main",
    )(
        kept(threshold.reshape(1, FREQS)),
        kept(fire_times),
        kept(rcv_delay),
        kept(record),
        gathered,
        split,
        full,
    )
    returned = lax.all_to_all(
        updated.reshape(PARTS, OWN, NT), "shot", split_axis=0, concat_axis=0, tiled=True
    )
    return pl.pallas_call(
        unpack_kernel,
        out_shape=jax.ShapeDtypeStruct((OWN, PARTS, NT), jnp.bfloat16),
        in_specs=[vmem()] * 2,
        out_specs=hbm(),
        scratch_shapes=[
            pltpu.VMEM((OWN, PARTS, NT), jnp.bfloat16),
            pltpu.SemaphoreType.DMA((4,)),
        ],
        compiler_params=PARAMS,
        name="unpack",
    )(returned, window)


def solution(mesh):
    in_specs = (P("shot", "rcv", None), P("rcv", "shot"), P("shot"), P("rcv"), P())
    out_specs = P("shot", "rcv", None)
    return jax.shard_map(shards, mesh=mesh, in_specs=in_specs, out_specs=out_specs, check_vma=False)
```

time: 40.1 us -> 38.5 us (0.960)
  blocking collectives: 33.7 us -> 32.4 us
    all_to_all x1, blocking collectives: 20.3 us -> 19 us  [shards(): lax.all_to_all(packed, 'shot', split_axis=0, concat_axis=0, tiled=True)]
where the time goes in v3:
time: 38.5 us; the launch traced here: 38.3 us
  blocking collectives  32.4 us (84%)
  Pallas kernels  5.86 us (15%)
    all_to_all x1, blocking collectives, shards(): lax.all_to_all(packed, 'shot', split_axis=0, concat_axis=0, tiled=True)  19 us
    all_to_all x1, blocking collectives, shards(): lax.all_to_all(updated.reshape(PARTS, OWN, NT), 'shot', split_axis=0, con...  13.5 us
    pallas_call x1, Pallas kernels, shards(): pl.pallas_call(main_kernel, out_shape=[jax.ShapeDtypeStruct((SHOTS, NT),...  3.2 us
    pallas_call x1, Pallas kernels, shards(): pl.pallas_call(pack_kernel, out_shape=jax.ShapeDtypeStruct((PARTS, PAYLOA...  1.61 us
    pallas_call x1, Pallas kernels, shards(): pl.pallas_call(unpack_kernel, out_shape=jax.ShapeDtypeStruct((OWN, PARTS,...  1.05 us

profile of v3, /device:TPU:160, one launch (start us, length us, event | category | flops | bytes accessed | tf_op | source)
XLA Modules:
  0.0 38.3 jit_solution(1882162801019989999)
XLA Ops:
  0.0 0.0 copy-start
  0.0 1.6 %pack.1 = bf16[16,136,128]{2,1,0:T(8,128)(2,1)S(1)} custom-call(s32[32]{0:T(128)} %fire_hbm.3, s32[16]{0:T(128)} %delay_hbm.3, bf16[16,2,16,512]{3,2,1,0:T(8,128)(2,1)} %bitcast.4, f32[16,4096]{1,0:T(8,128)} %record_hbm.3), custom_call_target="tpu_custom_call" | custom-call | tf_op jit(solution)/shard_map/pack/pallas_call | solution.py:337
  1.6 0.0 copy-start.1
  1.6 19.0 %all_to_all.10.data_ref = bf16[16,136,128]{2,1,0:T(8,128)(2,1)S(1)} all-to-all(bf16[16,136,128]{2,1,0:T(8,128)(2,1)S(1)} %pack.1), channel_id=1, replica_groups=mesh['shot'=16,'rcv'=16] {'shot'}, dimensions={0} | all-to-all | bytes 1114112 | tf_op jit(solution)/shard_map/all_to_all | solution.py:358
  20.6 0.0 copy-done
  20.6 0.0 copy-done.1
  20.6 3.2 %main.1 = (bf16[512,512]{1,0:T(8,128)(2,1)S(1)}, f32[32,16,512]{2,1,0:T(8,128)S(1)}) custom-call(f32[1,256]{1,0:T(1,128)} %bitcast.5, s32[32]{0:T(128)} %fire_hbm.3, s32[16]{0:T(128)} %delay_hbm.3, f32[16,4096]{1,0:T(8,128)} %record_hbm.3, bf16[16,136,128]{2,1,0:T(8,128)(2,1)S(1)} %all_to_all.10.data_ref, bf16[2,256,512]{2,1,0:T(8,128)(2,1)S(1)} %copy-done.1, ...), custom_call_target="tpu_custom_call" | custom-call | tf_op jit(solution)/shard_map/main/pallas_call | solution.py:360
  23.8 13.5 %all_to_all.11.data_ref = bf16[16,32,512]{2,1,0:T(8,128)(2,1)S(1)} all-to-all(bf16[16,32,512]{2,1,0:T(8,128)(2,1)S(1)} %bitcast.3), channel_id=1, replica_groups=mesh['shot'=16,'rcv'=16] {'shot'}, dimensions={0} | all-to-all | bytes 1048576 | tf_op jit(solution)/shard_map/all_to_all | solution.py:392
  37.3 1.1 %unpack.1 = bf16[32,16,512]{2,1,0:T(8,128)(2,1)} custom-call(bf16[16,32,512]{2,1,0:T(8,128)(2,1)S(1)} %all_to_all.11.data_ref, f32[32,16,512]{2,1,0:T(8,128)S(1)} %get-tuple-element.8.window_ref), custom_call_target="tpu_custom_call" | custom-call | tf_op jit(solution)/shard_map/unpack/pallas_call | solution.py:395
Async XLA Ops:
  0.0 20.6 %copy-start = (bf16[512,1024]{1,0:T(8,128)(2,1)S(1)}, bf16[512,1024]{1,0:T(8,128)(2,1)}, u32[]{:S(2)}) copy-start(bf16[512,1024]{1,0:T(8,128)(2,1)} %constant.5.clone.full_ref) | copy-start | bytes 3145732
  1.6 19.0 %copy-start.1 = (bf16[2,256,512]{2,1,0:T(8,128)(2,1)S(1)}, bf16[2,256,512]{2,1,0:T(8,128)(2,1)}, u32[]{:S(2)}) copy-start(bf16[2,256,512]{2,1,0:T(8,128)(2,1)} %constant.4.clone.split_ref) | copy-start | bytes 1572868

commit v4 on v3

--- a/solution.py
+++ b/solution.py
@@ -59,7 +59,10 @@
     delay_hbm,
     estimate_hbm,
     record_hbm,
+    threshold_hbm,
     out_ref,
+    own_ref,
+    level_ref,
     fire_ref,
     delay_ref,
     estimate_ref,
@@ -67,17 +70,10 @@
     small_sems,
     in_sems,
 ):
-    pieces = [(half, 0) for half in range(2)]
-    width = NT
-    arrivals = []
-    for at, (half, side) in enumerate(pieces):
-        arrivals.append(
-            pltpu.make_async_copy(
-                estimate_hbm.at[:, half],
-                estimate_ref.at[half],
-                in_sems.at[at],
-            )
-        )
+    arrivals = [
+        pltpu.make_async_copy(estimate_hbm.at[:, half], estimate_ref.at[half], in_sems.at[half])
+        for half in range(2)
+    ]
     fires = pltpu.make_async_copy(fire_hbm, fire_ref, small_sems.at[0])
     delays = pltpu.make_async_copy(delay_hbm, delay_ref, small_sems.at[1])
     heads = pltpu.make_async_copy(
@@ -87,27 +83,23 @@
     fires.start()
     delays.start()
     heads.start()
-    for arrival in arrivals[1:]:
-        arrival.start()
+    arrivals[1].start()
+    levels = pltpu.make_async_copy(threshold_hbm, level_ref, small_sems.at[3])
+    levels.start()
     swap = swap_table()
-    def turn(at):
-        half, side = pieces[at]
-        arrivals[at].wait()
-        traces = estimate_ref[half]
-        turned = dot(swap, traces.reshape(HALF * PARTS, width)).astype(jnp.bfloat16)
-        turned = turned.reshape(PARTS, HALF, width)
-        for block in range(4):
-            first = (4 * half + block) * HALF
-            out_ref[:, first : first + HALF, :] = turned[:, :, block * LANES : (block + 1) * LANES]
-
-    turn(0)
     lane = lax.broadcasted_iota(jnp.int32, (8, LANES), 1)
     row = lax.broadcasted_iota(jnp.int32, (8, LANES), 0)
+    which = lax.broadcasted_iota(jnp.int32, (PARTS, LANES), 0)
     offsets = jnp.zeros((8, LANES), jnp.int32)
+    delay = jnp.zeros((PARTS, LANES), jnp.int32)
     fires.wait()
     delays.wait()
+    for part in range(PARTS):
+        delay = jnp.where(which == part, delay_ref[part], delay)
     for shot in range(OWN):
-        offsets = jnp.where(lane == shot, fire_ref[shot] & (PERIOD - 1), offsets)
+        jitter = fire_ref[shot] & (PERIOD - 1)
+        offsets = jnp.where(lane == shot, jitter, offsets)
+        own_ref[shot] = delay + jitter
     heads.wait()
     for part in range(PARTS):
         rows = (offsets + delay_ref[part]).astype(jnp.float32)
@@ -115,7 +107,14 @@
             head = record_ref[part : part + 1, piece * LANES : (piece + 1) * LANES]
             rows = jnp.where(row == piece, jnp.broadcast_to(head, (8, LANES)), rows)
         out_ref[part, BLOCKS * OWN : BLOCKS * OWN + 8, :] = rows.astype(jnp.bfloat16)
-    turn(1)
+    levels.wait()
+    for half in range(2):
+        arrivals[half].wait()
+        turned = dot(swap, estimate_ref[half].reshape(HALF * PARTS, NT)).astype(jnp.bfloat16)
+        turned = turned.reshape(PARTS, HALF, NT)
+        for block in range(BLOCKS):
+            first = (half * BLOCKS + block) * HALF
+            out_ref[:, first : first + HALF, :] = turned[:, :, block * LANES : (block + 1) * LANES]
 
 
 def rotated(value, index):
@@ -139,10 +138,9 @@
 
 
 def main_kernel(
-    threshold_hbm,
-    fire_hbm,
-    delay_hbm,
-    record_hbm,
+    threshold_ref,
+    own_ref,
+    record_ref,
     data_ref,
     split_ref,
     full_ref,
@@ -154,30 +152,24 @@
     offset_ref,
     placed_ref,
     difference_ref,
-    threshold_ref,
-    fire_ref,
-    delay_ref,
-    record_ref,
-    sems,
 ):
-    pairs = [
-        (threshold_hbm, threshold_ref),
-        (fire_hbm, fire_ref),
-        (delay_hbm, delay_ref),
-        (record_hbm, record_ref),
-    ]
-    fetches = [
-        pltpu.make_async_copy(source, target, sems.at[at])
-        for at, (source, target) in enumerate(pairs)
-    ]
-    for fetch in fetches:
-        fetch.start()
     half_shots = SHOTS // 2
     data = data_ref
     lane = lax.broadcasted_iota(jnp.int32, (OWN, LANES), 1)
     row = lax.broadcasted_iota(jnp.int32, (OWN, LANES), 0)
 
-    waves = []
+    wide = lane[:PARTS]
+
+    def record_window(shot):
+        rows = [
+            record_ref[:, piece * LANES : (piece + 1) * LANES]
+            if RIM <= piece < OWN
+            else jnp.zeros((PARTS, LANES), jnp.float32)
+            for piece in range(shot, shot + RIM)
+        ]
+        for block, value in enumerate(read_windows(rows, own_ref[shot], wide)):
+            window_ref[shot, :, block * LANES : (block + 1) * LANES] = 0.5 * value
+
     for half in range(2):
         traces = jnp.concatenate(
             [
@@ -192,19 +184,10 @@
         stack_ref[half, :half_shots, FREQS:] = imag
         stack_ref[half, half_shots:, :FREQS] = imag
         stack_ref[half, half_shots:, FREQS:] = -real
-        waves.append(dot(split_ref[half], stack_ref[half]))
-
-    first = BLOCKS * OWN
-    picked = []
-    for part in range(PARTS):
-        rows = data[part, first : first + 8, :].astype(jnp.float32)
-        rows = jnp.broadcast_to(rows[7:8, :], (OWN, LANES))
-        picked.append(jnp.where(lane == row, rows, 0.0).astype(jnp.bfloat16))
-    ones = jnp.ones((LANES, LANES), jnp.bfloat16)
-    offset_ref[...] = dot(jnp.concatenate(picked, axis=0), ones).astype(jnp.int32)
-
-    for fetch in fetches:
-        fetch.wait()
+        for shot in range(half * HALF, half * HALF + HALF):
+            record_window(shot)
+
+    waves = [dot(split_ref[half], stack_ref[half]) for half in range(2)]
     freq = lax.broadcasted_iota(jnp.int32, (1, FREQS), 1)
     weight = jnp.where(freq == 0, 1.0, 2.0).astype(jnp.float32)
     level = weight * threshold_ref[...]
@@ -222,25 +205,7 @@
         shrunk_ref[here, FREQS:] = less
         shrunk_ref[there, FREQS:] = -real
 
-    wide = lax.broadcasted_iota(jnp.int32, (PARTS, LANES), 1)
-    which = lax.broadcasted_iota(jnp.int32, (PARTS, LANES), 0)
-    delay = jnp.zeros((PARTS, LANES), jnp.int32)
-    for part in range(PARTS):
-        delay = jnp.where(which == part, delay_ref[part], delay)
-
-    def record_window(shot):
-        rows = [
-            record_ref[:, piece * LANES : (piece + 1) * LANES]
-            if RIM <= piece < OWN
-            else jnp.zeros((PARTS, LANES), jnp.float32)
-            for piece in range(shot, shot + RIM)
-        ]
-        offset = delay + (fire_ref[shot] & (PERIOD - 1))
-        for block, value in enumerate(read_windows(rows, offset, wide)):
-            window_ref[shot, :, block * LANES : (block + 1) * LANES] = 0.5 * value
-
     step = OWN
-    zero = jnp.zeros((step, LANES), jnp.float32)
 
     def place(start):
         offset = offset_ref[start : start + step, :]
@@ -252,11 +217,16 @@
             )
             for block in range(BLOCKS)
         ]
-        turned = [zero, zero] + turned + [zero, zero]
-        for piece in range(RIM):
-            placed_ref[piece, 8 + start : 8 + start + step, :] = jnp.where(
-                near, turned[piece + 2], jnp.where(far, turned[piece + 1], turned[piece])
-            )
+        pieces = [
+            jnp.where(near, turned[0], 0.0),
+            jnp.where(near, turned[1], jnp.where(far, turned[0], 0.0)),
+            jnp.where(near, turned[2], jnp.where(far, turned[1], turned[0])),
+            jnp.where(near, turned[3], jnp.where(far, turned[2], turned[1])),
+            jnp.where(near, 0.0, jnp.where(far, turned[3], turned[2])),
+            jnp.where(far, 0.0, turned[3]),
+        ]
+        for at, piece in enumerate(pieces):
+            placed_ref[at, 8 + start : 8 + start + step, :] = piece
 
     def subtract(start):
         total = placed_ref[0, 8 + start : 8 + start + step, :]
@@ -276,23 +246,34 @@
                 denoised_ref[start : start + step, lanes] + value
             ).astype(jnp.bfloat16)
 
+    for part in range(PARTS):
+        rows = data[part, BLOCKS * OWN : BLOCKS * OWN + 8, :].astype(jnp.float32)
+        rows = jnp.broadcast_to(rows[RIM + 1 :, :].astype(jnp.int32), (OWN, LANES))
+        offset_ref[part * OWN : (part + 1) * OWN, :] = rotated(rows, row)
+
     inverse = jnp.concatenate([full_ref[:FREQS, :SHOTS], full_ref[:FREQS, SHOTS:]], axis=0)
     part_shots = SHOTS // CHUNKS
+    steps = SHOTS // step
+    subtracted, finished = 1, 1
     for part in range(CHUNKS):
         shots = slice(part * part_shots, (part + 1) * part_shots)
         back = dot(full_ref[shots, :], shrunk_ref[...]).astype(jnp.bfloat16)
         denoised_ref[shots, :] = dot(back, inverse)
-        for shot in range(part * OWN // CHUNKS, (part + 1) * OWN // CHUNKS):
-            record_window(shot)
         for start in range(part * part_shots, (part + 1) * part_shots, step):
             place(start)
+        ready = (part + 1) * steps // CHUNKS
+        for at in range(subtracted, ready):
+            subtract(at * step)
+        subtracted = ready
+        for at in range(finished, ready - 1):
+            finish(at * step)
+        finished = ready - 1
     for piece in range(1, RIM):
         placed_ref[piece, 0:8, :] = placed_ref[piece, SHOTS : SHOTS + 8, :]
-    for start in range(0, SHOTS, step):
-        subtract(start)
+    subtract(0)
     difference_ref[SHOTS : SHOTS + 8, :] = difference_ref[0:8, :]
-    for start in range(0, SHOTS, step):
-        finish(start)
+    finish(SHOTS - step)
+    finish(0)
 
 
 def unpack_kernel(data_ref, window_ref, out_hbm, out_ref, sems):
@@ -334,17 +315,21 @@
 
 
 def shards(estimate, record, fire_times, rcv_delay, threshold):
-    packed = pl.pallas_call(
+    packed, own, levels = pl.pallas_call(
         pack_kernel,
-        out_shape=jax.ShapeDtypeStruct((PARTS, PAYLOAD, LANES), jnp.bfloat16),
-        in_specs=[hbm()] * 4,
-        out_specs=vmem(),
+        out_shape=[
+            jax.ShapeDtypeStruct((PARTS, PAYLOAD, LANES), jnp.bfloat16),
+            jax.ShapeDtypeStruct((OWN, PARTS, LANES), jnp.int32),
+            jax.ShapeDtypeStruct((1, FREQS), jnp.float32),
+        ],
+        in_specs=[hbm()] * 5,
+        out_specs=[vmem()] * 3,
         scratch_shapes=[
             pltpu.SMEM((OWN,), jnp.int32),
             pltpu.SMEM((PARTS,), jnp.int32),
             pltpu.VMEM((2, HALF, PARTS, NT), jnp.bfloat16),
             pltpu.VMEM((PARTS, RIM * LANES), jnp.float32),
-            pltpu.SemaphoreType.DMA((3,)),
+            pltpu.SemaphoreType.DMA((4,)),
             pltpu.SemaphoreType.DMA((2,)),
         ],
         compiler_params=PARAMS,
@@ -354,6 +339,7 @@
         kept(rcv_delay),
         kept(estimate.reshape(HALF, 2, PARTS, NT)),
         kept(record),
+        kept(threshold.reshape(1, FREQS)),
     )
     gathered = lax.all_to_all(packed, "shot", split_axis=0, concat_axis=0, tiled=True)
     split, full = (jnp.asarray(table) for table in tables())
@@ -363,7 +349,7 @@
             jax.ShapeDtypeStruct((SHOTS, NT), jnp.bfloat16),
             jax.ShapeDtypeStruct((OWN, PARTS, NT), jnp.float32),
         ],
-        in_specs=[hbm()] * 4 + [vmem()] * 3,
+        in_specs=[vmem()] * 6,
         out_specs=[vmem()] * 2,
         scratch_shapes=[
             pltpu.VMEM((2, SHOTS, NT), jnp.bfloat16),
@@ -372,19 +358,13 @@
             pltpu.VMEM((SHOTS, LANES), jnp.int32),
             pltpu.VMEM((RIM, SHOTS + 8, LANES), jnp.float32),
             pltpu.VMEM((SHOTS + 8, LANES), jnp.float32),
-            pltpu.VMEM((1, FREQS), jnp.float32),
-            pltpu.SMEM((OWN,), jnp.int32),
-            pltpu.SMEM((PARTS,), jnp.int32),
-            pltpu.VMEM((PARTS, OWN * LANES), jnp.float32),
-            pltpu.SemaphoreType.DMA((4,)),
         ],
         compiler_params=PARAMS,
         name="main",
     )(
-        kept(threshold.reshape(1, FREQS)),
-        kept(fire_times),
-        kept(rcv_delay),
-        kept(record),
+        levels,
+        own,
+        record,
         gathered,
         split,
         full,

time: 38.5 us -> 38.1 us (0.990)
  Pallas kernels: 5.86 us -> 5.41 us
    pallas_call x1, Pallas kernels: 3.2 us -> 2.8 us  [shards(): pl.pallas_call(main_kernel, out_shape=[jax.ShapeDtypeStruct((SHOTS, NT),...]
where the time goes in v4:
time: 38.1 us; the launch traced here: 37.9 us
  blocking collectives  32.4 us (85%)
  Pallas kernels  5.41 us (14%)
    all_to_all x1, blocking collectives, shards(): lax.all_to_all(packed, 'shot', split_axis=0, concat_axis=0, tiled=True)  19 us
    all_to_all x1, blocking collectives, shards(): lax.all_to_all(updated.reshape(PARTS, OWN, NT), 'shot', split_axis=0, con...  13.5 us
    pallas_call x1, Pallas kernels, shards(): pl.pallas_call(main_kernel, out_shape=[jax.ShapeDtypeStruct((SHOTS, NT),...  2.8 us
    pallas_call x1, Pallas kernels, shards(): pl.pallas_call(pack_kernel, out_shape=[jax.ShapeDtypeStruct((PARTS, PAYLO...  1.55 us
    pallas_call x1, Pallas kernels, shards(): pl.pallas_call(unpack_kernel, out_shape=jax.ShapeDtypeStruct((OWN, PARTS,...  1.05 us

profile of v4, /device:TPU:160, one launch (start us, length us, event | category | flops | bytes accessed | tf_op | source)
XLA Modules:
  0.0 37.9 jit_solution(4702038981433314812)
XLA Ops:
  0.0 0.0 copy-start
  0.0 1.6 %pack.1 = (bf16[16,136,128]{2,1,0:T(8,128)(2,1)S(1)}, s32[32,16,128]{2,1,0:T(8,128)S(1)}, f32[1,256]{1,0:T(1,128)S(1)}) custom-call(s32[32]{0:T(128)} %fire_hbm.1, s32[16]{0:T(128)} %delay_hbm.1, bf16[16,2,16,512]{3,2,1,0:T(8,128)(2,1)} %bitcast.4, f32[16,4096]{1,0:T(8,128)} %record_ref.1, f32[1,256]{1,0:T(1,128)} %bitcast.5), custom_call_target="tpu_custom_call" | custom-call | tf_op jit(solution)/shard_map/pack/pallas_call | solution.py:318
  1.6 0.0 copy-start.1
  1.6 0.0 copy-start.2
  1.6 19.0 %all_to_all.10.data_ref = bf16[16,136,128]{2,1,0:T(8,128)(2,1)S(1)} all-to-all(bf16[16,136,128]{2,1,0:T(8,128)(2,1)S(1)} %get-tuple-element.12), channel_id=1, replica_groups=mesh['shot'=16,'rcv'=16] {'shot'}, dimensions={0} | all-to-all | bytes 1114112 | tf_op jit(solution)/shard_map/all_to_all | solution.py:344
  20.6 0.0 copy-done
  20.6 0.0 copy-done.1
  20.6 0.0 copy-done.2
  20.6 2.8 %main.1 = (bf16[512,512]{1,0:T(8,128)(2,1)S(1)}, f32[32,16,512]{2,1,0:T(8,128)S(1)}) custom-call(f32[1,256]{1,0:T(1,128)S(1)} %get-tuple-element.10.threshold_ref, s32[32,16,128]{2,1,0:T(8,128)S(1)} %get-tuple-element.11.own_ref, f32[16,4096]{1,0:T(8,128)S(1)} %copy-done.1, bf16[16,136,128]{2,1,0:T(8,128)(2,1)S(1)} %all_to_all.10.data_ref, ...), custom_call_target="tpu_custom_call" | custom-call | tf_op jit(solution)/shard_map/main/pallas_call | solution.py:346
  23.4 13.5 %all_to_all.11.data_ref = bf16[16,32,512]{2,1,0:T(8,128)(2,1)S(1)} all-to-all(bf16[16,32,512]{2,1,0:T(8,128)(2,1)S(1)} %bitcast.3), channel_id=1, replica_groups=mesh['shot'=16,'rcv'=16] {'shot'}, dimensions={0} | all-to-all | bytes 1048576 | tf_op jit(solution)/shard_map/all_to_all | solution.py:372
  36.9 1.1 %unpack.1 = bf16[32,16,512]{2,1,0:T(8,128)(2,1)} custom-call(bf16[16,32,512]{2,1,0:T(8,128)(2,1)S(1)} %all_to_all.11.data_ref, f32[32,16,512]{2,1,0:T(8,128)S(1)} %get-tuple-element.14.window_ref), custom_call_target="tpu_custom_call" | custom-call | tf_op jit(solution)/shard_map/unpack/pallas_call | solution.py:375
Async XLA Ops:
  0.0 20.6 %copy-start = (bf16[512,1024]{1,0:T(8,128)(2,1)S(1)}, bf16[512,1024]{1,0:T(8,128)(2,1)}, u32[]{:S(2)}) copy-start(bf16[512,1024]{1,0:T(8,128)(2,1)} %constant.5.clone.full_ref) | copy-start | bytes 3145732
  1.6 19.0 %copy-start.1 = (f32[16,4096]{1,0:T(8,128)S(1)}, f32[16,4096]{1,0:T(8,128)}, u32[]{:S(2)}) copy-start(f32[16,4096]{1,0:T(8,128)} %record_ref.1) | copy-start | bytes 786436
  1.6 19.0 %copy-start.2 = (bf16[2,256,512]{2,1,0:T(8,128)(2,1)S(1)}, bf16[2,256,512]{2,1,0:T(8,128)(2,1)}, u32[]{:S(2)}) copy-start(bf16[2,256,512]{2,1,0:T(8,128)(2,1)} %constant.4.clone.split_ref) | copy-start | bytes 1572868

commit v5 on v4

--- a/solution.py
+++ b/solution.py
@@ -45,13 +45,6 @@
 
 def dot(a, b):
     return jnp.dot(a, b, preferred_element_type=jnp.float32)
-
-
-def swap_table():
-    row = lax.broadcasted_iota(jnp.int32, (256, 256), 0)
-    column = lax.broadcasted_iota(jnp.int32, (256, 256), 1)
-    source = (row & 15) * 16 + (row >> 4)
-    return jnp.where(column == source, 1.0, 0.0).astype(jnp.bfloat16)
 
 
 def pack_kernel(
@@ -80,13 +73,12 @@
         record_hbm.at[:, pl.ds(0, RIM * LANES)], record_ref, small_sems.at[2]
     )
     arrivals[0].start()
+    arrivals[1].start()
     fires.start()
     delays.start()
     heads.start()
-    arrivals[1].start()
     levels = pltpu.make_async_copy(threshold_hbm, level_ref, small_sems.at[3])
     levels.start()
-    swap = swap_table()
     lane = lax.broadcasted_iota(jnp.int32, (8, LANES), 1)
     row = lax.broadcasted_iota(jnp.int32, (8, LANES), 0)
     which = lax.broadcasted_iota(jnp.int32, (PARTS, LANES), 0)
@@ -110,8 +102,7 @@
     levels.wait()
     for half in range(2):
         arrivals[half].wait()
-        turned = dot(swap, estimate_ref[half].reshape(HALF * PARTS, NT)).astype(jnp.bfloat16)
-        turned = turned.reshape(PARTS, HALF, NT)
+        turned = jnp.swapaxes(estimate_ref[half], 0, 1)
         for block in range(BLOCKS):
             first = (half * BLOCKS + block) * HALF
             out_ref[:, first : first + HALF, :] = turned[:, :, block * LANES : (block + 1) * LANES]
@@ -277,16 +268,15 @@
 
 
 def unpack_kernel(data_ref, window_ref, out_hbm, out_ref, sems):
-    swap = swap_table()
     width = NT // 2
     copies = []
     for half in range(2):
         shots = slice(half * HALF, (half + 1) * HALF)
         for side in range(2):
             lanes = slice(side * width, (side + 1) * width)
-            rows = data_ref[:, shots, lanes].reshape(PARTS * HALF, width)
+            rows = data_ref[:, shots, lanes]
             out_ref[shots, :, lanes] = (
-                dot(swap, rows).reshape(HALF, PARTS, width) + window_ref[shots, :, lanes]
+                jnp.swapaxes(rows, 0, 1).astype(jnp.float32) + window_ref[shots, :, lanes]
             ).astype(jnp.bfloat16)
             place = (pl.ds(half * HALF, HALF), slice(None), pl.ds(side * width, width))
             copies.append(

time: 38.1 us -> 37.7 us (0.990)
  Pallas kernels: 5.41 us -> 4.97 us
where the time goes in v5:
time: 37.7 us; the launch traced here: 37.5 us
  blocking collectives  32.5 us (86%)
  Pallas kernels  4.97 us (13%)
    all_to_all x1, blocking collectives, shards(): lax.all_to_all(packed, 'shot', split_axis=0, concat_axis=0, tiled=True)  19 us
    all_to_all x1, blocking collectives, shards(): lax.all_to_all(updated.reshape(PARTS, OWN, NT), 'shot', split_axis=0, con...  13.5 us
    pallas_call x1, Pallas kernels, shards(): pl.pallas_call(main_kernel, out_shape=[jax.ShapeDtypeStruct((SHOTS, NT),...  2.79 us
    pallas_call x1, Pallas kernels, shards(): pl.pallas_call(pack_kernel, out_shape=[jax.ShapeDtypeStruct((PARTS, PAYLO...  1.27 us
    pallas_call x1, Pallas kernels, shards(): pl.pallas_call(unpack_kernel, out_shape=jax.ShapeDtypeStruct((OWN, PARTS,...  0.91 us

profile of v5, /device:TPU:160, one launch (start us, length us, event | category | flops | bytes accessed | tf_op | source)
XLA Modules:
  0.0 37.5 jit_solution(1212144465087901407)
XLA Ops:
  0.0 0.0 copy-start
  0.0 1.3 %pack.1 = (bf16[16,136,128]{2,1,0:T(8,128)(2,1)S(1)}, s32[32,16,128]{2,1,0:T(8,128)S(1)}, f32[1,256]{1,0:T(1,128)S(1)}) custom-call(s32[32]{0:T(128)} %fire_hbm.1, s32[16]{0:T(128)} %delay_hbm.1, bf16[16,2,16,512]{3,2,1,0:T(8,128)(2,1)} %bitcast.4, f32[16,4096]{1,0:T(8,128)} %record_ref.1, f32[1,256]{1,0:T(1,128)} %bitcast.5), custom_call_target="tpu_custom_call" | custom-call | tf_op jit(solution)/shard_map/pack/pallas_call | solution.py:308
  1.3 0.0 copy-start.1
  1.3 0.0 copy-start.2
  1.3 19.0 %all_to_all.10.data_ref = bf16[16,136,128]{2,1,0:T(8,128)(2,1)S(1)} all-to-all(bf16[16,136,128]{2,1,0:T(8,128)(2,1)S(1)} %get-tuple-element.12), channel_id=1, replica_groups=mesh['shot'=16,'rcv'=16] {'shot'}, dimensions={0} | all-to-all | bytes 1114112 | tf_op jit(solution)/shard_map/all_to_all | solution.py:334
  20.3 0.0 copy-done
  20.3 0.0 copy-done.1
  20.3 0.0 copy-done.2
  20.3 2.8 %main.1 = (bf16[512,512]{1,0:T(8,128)(2,1)S(1)}, f32[32,16,512]{2,1,0:T(8,128)S(1)}) custom-call(f32[1,256]{1,0:T(1,128)S(1)} %get-tuple-element.10.threshold_ref, s32[32,16,128]{2,1,0:T(8,128)S(1)} %get-tuple-element.11.own_ref, f32[16,4096]{1,0:T(8,128)S(1)} %copy-done.1, bf16[16,136,128]{2,1,0:T(8,128)(2,1)S(1)} %all_to_all.10.data_ref, ...), custom_call_target="tpu_custom_call" | custom-call | tf_op jit(solution)/shard_map/main/pallas_call | solution.py:336
  23.1 13.5 %all_to_all.11.data_ref = bf16[16,32,512]{2,1,0:T(8,128)(2,1)S(1)} all-to-all(bf16[16,32,512]{2,1,0:T(8,128)(2,1)S(1)} %bitcast.3), channel_id=1, replica_groups=mesh['shot'=16,'rcv'=16] {'shot'}, dimensions={0} | all-to-all | bytes 1048576 | tf_op jit(solution)/shard_map/all_to_all | solution.py:362
  36.6 0.9 %unpack.1 = bf16[32,16,512]{2,1,0:T(8,128)(2,1)} custom-call(bf16[16,32,512]{2,1,0:T(8,128)(2,1)S(1)} %all_to_all.11.data_ref, f32[32,16,512]{2,1,0:T(8,128)S(1)} %get-tuple-element.14.window_ref), custom_call_target="tpu_custom_call" | custom-call | tf_op jit(solution)/shard_map/unpack/pallas_call | solution.py:365
Async XLA Ops:
  0.0 20.3 %copy-start = (bf16[512,1024]{1,0:T(8,128)(2,1)S(1)}, bf16[512,1024]{1,0:T(8,128)(2,1)}, u32[]{:S(2)}) copy-start(bf16[512,1024]{1,0:T(8,128)(2,1)} %constant.5.clone.full_ref) | copy-start | bytes 3145732
  1.3 19.0 %copy-start.1 = (f32[16,4096]{1,0:T(8,128)S(1)}, f32[16,4096]{1,0:T(8,128)}, u32[]{:S(2)}) copy-start(f32[16,4096]{1,0:T(8,128)} %record_ref.1) | copy-start | bytes 786436
  1.3 19.0 %copy-start.2 = (bf16[2,256,512]{2,1,0:T(8,128)(2,1)S(1)}, bf16[2,256,512]{2,1,0:T(8,128)(2,1)}, u32[]{:S(2)}) copy-start(bf16[2,256,512]{2,1,0:T(8,128)(2,1)} %constant.4.clone.split_ref) | copy-start | bytes 1572868

commit v6 on v5

--- a/solution.py
+++ b/solution.py
@@ -92,6 +92,14 @@
         jitter = fire_ref[shot] & (PERIOD - 1)
         offsets = jnp.where(lane == shot, jitter, offsets)
         own_ref[shot] = delay + jitter
+    def turn(half):
+        arrivals[half].wait()
+        turned = jnp.swapaxes(estimate_ref[half], 0, 1)
+        for block in range(BLOCKS):
+            first = (half * BLOCKS + block) * HALF
+            out_ref[:, first : first + HALF, :] = turned[:, :, block * LANES : (block + 1) * LANES]
+
+    turn(0)
     heads.wait()
     for part in range(PARTS):
         rows = (offsets + delay_ref[part]).astype(jnp.float32)
@@ -99,13 +107,8 @@
             head = record_ref[part : part + 1, piece * LANES : (piece + 1) * LANES]
             rows = jnp.where(row == piece, jnp.broadcast_to(head, (8, LANES)), rows)
         out_ref[part, BLOCKS * OWN : BLOCKS * OWN + 8, :] = rows.astype(jnp.bfloat16)
+    turn(1)
     levels.wait()
-    for half in range(2):
-        arrivals[half].wait()
-        turned = jnp.swapaxes(estimate_ref[half], 0, 1)
-        for block in range(BLOCKS):
-            first = (half * BLOCKS + block) * HALF
-            out_ref[:, first : first + HALF, :] = turned[:, :, block * LANES : (block + 1) * LANES]
 
 
 def rotated(value, index):

time: 37.7 us -> 37.7 us (level)
  no operation moved by 1% of the time
where the time goes in v6:
time: 37.7 us; the launch traced here: 37.5 us
  blocking collectives  32.5 us (86%)
  Pallas kernels  4.98 us (13%)
    all_to_all x1, blocking collectives, shards(): lax.all_to_all(packed, 'shot', split_axis=0, concat_axis=0, tiled=True)  19 us
    all_to_all x1, blocking collectives, shards(): lax.all_to_all(updated.reshape(PARTS, OWN, NT), 'shot', split_axis=0, con...  13.5 us
    pallas_call x1, Pallas kernels, shards(): pl.pallas_call(main_kernel, out_shape=[jax.ShapeDtypeStruct((SHOTS, NT),...  2.79 us
    pallas_call x1, Pallas kernels, shards(): pl.pallas_call(pack_kernel, out_shape=[jax.ShapeDtypeStruct((PARTS, PAYLO...  1.29 us
    pallas_call x1, Pallas kernels, shards(): pl.pallas_call(unpack_kernel, out_shape=jax.ShapeDtypeStruct((OWN, PARTS,...  0.91 us

profile of v6, /device:TPU:160, one launch (start us, length us, event | category | flops | bytes accessed | tf_op | source)
XLA Modules:
  0.0 37.5 jit_solution(16017091447320280132)
XLA Ops:
  0.0 0.0 copy-start
  0.0 1.3 %pack.1 = (bf16[16,136,128]{2,1,0:T(8,128)(2,1)S(1)}, s32[32,16,128]{2,1,0:T(8,128)S(1)}, f32[1,256]{1,0:T(1,128)S(1)}) custom-call(s32[32]{0:T(128)} %fire_hbm.1, s32[16]{0:T(128)} %delay_hbm.1, bf16[16,2,16,512]{3,2,1,0:T(8,128)(2,1)} %bitcast.4, f32[16,4096]{1,0:T(8,128)} %record_ref.1, f32[1,256]{1,0:T(1,128)} %bitcast.5), custom_call_target="tpu_custom_call" | custom-call | tf_op jit(solution)/shard_map/pack/pallas_call | solution.py:311
  1.3 0.0 copy-start.1
  1.3 0.0 copy-start.2
  1.3 19.0 %all_to_all.10.data_ref = bf16[16,136,128]{2,1,0:T(8,128)(2,1)S(1)} all-to-all(bf16[16,136,128]{2,1,0:T(8,128)(2,1)S(1)} %get-tuple-element.12), channel_id=1, replica_groups=mesh['shot'=16,'rcv'=16] {'shot'}, dimensions={0} | all-to-all | bytes 1114112 | tf_op jit(solution)/shard_map/all_to_all | solution.py:337
  20.3 0.0 copy-done
  20.3 0.0 copy-done.1
  20.3 0.0 copy-done.2
  20.3 2.8 %main.1 = (bf16[512,512]{1,0:T(8,128)(2,1)S(1)}, f32[32,16,512]{2,1,0:T(8,128)S(1)}) custom-call(f32[1,256]{1,0:T(1,128)S(1)} %get-tuple-element.10.threshold_ref, s32[32,16,128]{2,1,0:T(8,128)S(1)} %get-tuple-element.11.own_ref, f32[16,4096]{1,0:T(8,128)S(1)} %copy-done.1, bf16[16,136,128]{2,1,0:T(8,128)(2,1)S(1)} %all_to_all.10.data_ref, ...), custom_call_target="tpu_custom_call" | custom-call | tf_op jit(solution)/shard_map/main/pallas_call | solution.py:339
  23.1 13.5 %all_to_all.11.data_ref = bf16[16,32,512]{2,1,0:T(8,128)(2,1)S(1)} all-to-all(bf16[16,32,512]{2,1,0:T(8,128)(2,1)S(1)} %bitcast.3), channel_id=1, replica_groups=mesh['shot'=16,'rcv'=16] {'shot'}, dimensions={0} | all-to-all | bytes 1048576 | tf_op jit(solution)/shard_map/all_to_all | solution.py:365
  36.6 0.9 %unpack.1 = bf16[32,16,512]{2,1,0:T(8,128)(2,1)} custom-call(bf16[16,32,512]{2,1,0:T(8,128)(2,1)S(1)} %all_to_all.11.data_ref, f32[32,16,512]{2,1,0:T(8,128)S(1)} %get-tuple-element.14.window_ref), custom_call_target="tpu_custom_call" | custom-call | tf_op jit(solution)/shard_map/unpack/pallas_call | solution.py:368
Async XLA Ops:
  0.0 20.3 %copy-start = (bf16[512,1024]{1,0:T(8,128)(2,1)S(1)}, bf16[512,1024]{1,0:T(8,128)(2,1)}, u32[]{:S(2)}) copy-start(bf16[512,1024]{1,0:T(8,128)(2,1)} %constant.5.clone.full_ref) | copy-start | bytes 3145732
  1.3 19.0 %copy-start.1 = (f32[16,4096]{1,0:T(8,128)S(1)}, f32[16,4096]{1,0:T(8,128)}, u32[]{:S(2)}) copy-start(f32[16,4096]{1,0:T(8,128)} %record_ref.1) | copy-start | bytes 786436
  1.3 19.0 %copy-start.2 = (bf16[2,256,512]{2,1,0:T(8,128)(2,1)S(1)}, bf16[2,256,512]{2,1,0:T(8,128)(2,1)}, u32[]{:S(2)}) copy-start(bf16[2,256,512]{2,1,0:T(8,128)(2,1)} %constant.4.clone.split_ref) | copy-start | bytes 1572868

commit v7 on v5

--- a/solution.py
+++ b/solution.py
@@ -249,7 +249,9 @@
     for part in range(CHUNKS):
         shots = slice(part * part_shots, (part + 1) * part_shots)
         back = dot(full_ref[shots, :], shrunk_ref[...]).astype(jnp.bfloat16)
-        denoised_ref[shots, :] = dot(back, inverse)
+        denoised_ref[shots, :] = dot(back[:, :FREQS], full_ref[:FREQS, :SHOTS]) + dot(
+            back[:, FREQS:], full_ref[:FREQS, SHOTS:]
+        )
         for start in range(part * part_shots, (part + 1) * part_shots, step):
             place(start)
         ready = (part + 1) * steps // CHUNKS

time: 37.7 us -> 37.7 us (level)
  no operation moved by 1% of the time
where the time goes in v7:
time: 37.7 us; the launch traced here: 37.5 us
  blocking collectives  32.5 us (86%)
  Pallas kernels  4.99 us (13%)
    all_to_all x1, blocking collectives, shards(): lax.all_to_all(packed, 'shot', split_axis=0, concat_axis=0, tiled=True)  19 us
    all_to_all x1, blocking collectives, shards(): lax.all_to_all(updated.reshape(PARTS, OWN, NT), 'shot', split_axis=0, con...  13.5 us
    pallas_call x1, Pallas kernels, shards(): pl.pallas_call(main_kernel, out_shape=[jax.ShapeDtypeStruct((SHOTS, NT),...  2.81 us
    pallas_call x1, Pallas kernels, shards(): pl.pallas_call(pack_kernel, out_shape=[jax.ShapeDtypeStruct((PARTS, PAYLO...  1.27 us
    pallas_call x1, Pallas kernels, shards(): pl.pallas_call(unpack_kernel, out_shape=jax.ShapeDtypeStruct((OWN, PARTS,...  0.91 us

profile of v7, /device:TPU:160, one launch (start us, length us, event | category | flops | bytes accessed | tf_op | source)
XLA Modules:
  0.0 37.5 jit_solution(3281561091195391835)
XLA Ops:
  0.0 0.0 copy-start
  0.0 1.3 %pack.1 = (bf16[16,136,128]{2,1,0:T(8,128)(2,1)S(1)}, s32[32,16,128]{2,1,0:T(8,128)S(1)}, f32[1,256]{1,0:T(1,128)S(1)}) custom-call(s32[32]{0:T(128)} %fire_hbm.1, s32[16]{0:T(128)} %delay_hbm.1, bf16[16,2,16,512]{3,2,1,0:T(8,128)(2,1)} %bitcast.4, f32[16,4096]{1,0:T(8,128)} %record_ref.1, f32[1,256]{1,0:T(1,128)} %bitcast.5), custom_call_target="tpu_custom_call" | custom-call | tf_op jit(solution)/shard_map/pack/pallas_call | solution.py:310
  1.3 0.0 copy-start.1
  1.3 0.0 copy-start.2
  1.3 19.0 %all_to_all.10.data_ref = bf16[16,136,128]{2,1,0:T(8,128)(2,1)S(1)} all-to-all(bf16[16,136,128]{2,1,0:T(8,128)(2,1)S(1)} %get-tuple-element.12), channel_id=1, replica_groups=mesh['shot'=16,'rcv'=16] {'shot'}, dimensions={0} | all-to-all | bytes 1114112 | tf_op jit(solution)/shard_map/all_to_all | solution.py:336
  20.3 0.0 copy-done
  20.3 0.0 copy-done.1
  20.3 0.0 copy-done.2
  20.3 2.8 %main.1 = (bf16[512,512]{1,0:T(8,128)(2,1)S(1)}, f32[32,16,512]{2,1,0:T(8,128)S(1)}) custom-call(f32[1,256]{1,0:T(1,128)S(1)} %get-tuple-element.10.threshold_ref, s32[32,16,128]{2,1,0:T(8,128)S(1)} %get-tuple-element.11.own_ref, f32[16,4096]{1,0:T(8,128)S(1)} %copy-done.1, bf16[16,136,128]{2,1,0:T(8,128)(2,1)S(1)} %all_to_all.10.data_ref, ...), custom_call_target="tpu_custom_call" | custom-call | tf_op jit(solution)/shard_map/main/pallas_call | solution.py:338
  23.1 13.5 %all_to_all.11.data_ref = bf16[16,32,512]{2,1,0:T(8,128)(2,1)S(1)} all-to-all(bf16[16,32,512]{2,1,0:T(8,128)(2,1)S(1)} %bitcast.3), channel_id=1, replica_groups=mesh['shot'=16,'rcv'=16] {'shot'}, dimensions={0} | all-to-all | bytes 1048576 | tf_op jit(solution)/shard_map/all_to_all | solution.py:364
  36.6 0.9 %unpack.1 = bf16[32,16,512]{2,1,0:T(8,128)(2,1)} custom-call(bf16[16,32,512]{2,1,0:T(8,128)(2,1)S(1)} %all_to_all.11.data_ref, f32[32,16,512]{2,1,0:T(8,128)S(1)} %get-tuple-element.14.window_ref), custom_call_target="tpu_custom_call" | custom-call | tf_op jit(solution)/shard_map/unpack/pallas_call | solution.py:367
Async XLA Ops:
  0.0 20.3 %copy-start = (bf16[512,1024]{1,0:T(8,128)(2,1)S(1)}, bf16[512,1024]{1,0:T(8,128)(2,1)}, u32[]{:S(2)}) copy-start(bf16[512,1024]{1,0:T(8,128)(2,1)} %constant.5.clone.full_ref) | copy-start | bytes 3145732
  1.3 19.0 %copy-start.1 = (f32[16,4096]{1,0:T(8,128)S(1)}, f32[16,4096]{1,0:T(8,128)}, u32[]{:S(2)}) copy-start(f32[16,4096]{1,0:T(8,128)} %record_ref.1) | copy-start | bytes 786436
  1.3 19.0 %copy-start.2 = (bf16[2,256,512]{2,1,0:T(8,128)(2,1)S(1)}, bf16[2,256,512]{2,1,0:T(8,128)(2,1)}, u32[]{:S(2)}) copy-start(bf16[2,256,512]{2,1,0:T(8,128)(2,1)} %constant.4.clone.split_ref) | copy-start | bytes 1572868
